TPU v7x, 128 devices: a whole 4x4x4 slice. The times are simulated.
128 devices in a mesh: layer: 8 (over z, core), energy: 4 (over y), momentum: 4 (over x).
Axes of the slice: x: 4, y: 4, z: 4, core: 2. Of those that a mesh axis runs over, the one named last changes fastest.
Arguments:
- diag_blocks: float32 [4, 16, 4, 2, 384, 384], P('momentum', 'layer', 'energy'), may hold values from -1 to 5
- couplings: float32 [4, 16, 2, 384, 384], P('momentum', 'layer'), may hold values from -0.15625 to 0.15625
- phonon_matrix: float32 [4, 4], replicated, may hold values from -3 to 3
- mode_strength: float32 [3], replicated, may hold values from 0.5 to 2
- transfer_mode: int32 [4], replicated, may hold values from 0 to 2, as said below
- energy_offset: int32 [3], replicated, may hold values from 0 to 1, as said below
Outputs:
- self_energy: float32 [4, 8, 4, 2, 384, 384], P('momentum', 'layer', 'energy')
Inputs may be any that keep to these rules, and one draw needn't show every extreme that they name: `transfer_mode`: every one of the 3 modes is the mode of some transfer. `energy_offset`: some mode has offset 0 and some mode has offset 1.
All inputs are finite; a program needn't handle non-finite values.
Results may differ from a plain program's by a relative error of at most 0.00011.
Values sent between devices are 32-bit elements; how exact they have to be, the bound alone decides.
No kernel may reach another device: no remote copies, remote signals or barrier semaphores. Data moves between devices by JAX's collectives and lax.ppermute only.
A program may use at most 64 MiB of HBM per device.

v0:
```python
import jax
import jax.numpy as jnp
from jax import lax
from jax.experimental import pallas as pl
from jax.experimental.pallas import tpu as pltpu
from jax.sharding import PartitionSpec as P

F32 = jnp.float32
BF16 = jnp.bfloat16


def split(value):
    high = value.astype(BF16)
    return high, (value - high.astype(F32)).astype(BF16)


LANES = 128


def cut(at):
    return slice(LANES * at, LANES * (at + 1))


def pair(at):
    return slice(2 * LANES * at, 2 * LANES * (at + 1))


def real_of(at):
    return slice(2 * LANES * at, 2 * LANES * at + LANES)


def imag_of(at):
    return slice(2 * LANES * at + LANES, 2 * LANES * (at + 1))


def put_left(left, at, real, imag):
    for columns, part in ((real_of(at), real), (imag_of(at), imag)):
        for ref, value in zip(left, split(part)):
            ref[:, columns] = value


def put_right(right, at, real, imag):
    for ref, r, i in zip(right, split(real), split(imag)):
        minus = -i
        for k in range(real.shape[0] // LANES):
            rows = cut(k)
            ref[real_of(k), real_of(at)] = r[rows]
            ref[real_of(k), imag_of(at)] = i[rows]
            ref[imag_of(k), real_of(at)] = minus[rows]
            ref[imag_of(k), imag_of(at)] = r[rows]


def product(left, right, epilogue, fill=()):
    for at in range(right[0].shape[1] // (2 * LANES)):
        columns = pair(at)
        high = right[0][:, columns]
        lh = left[0][...]
        value = (
            jnp.dot(lh, high, preferred_element_type=F32)
            + jnp.dot(lh, right[1][:, columns], preferred_element_type=F32)
            + jnp.dot(left[1][...], high, preferred_element_type=F32)
        )
        if at < len(fill):
            fill[at]()
        epilogue(at, value[:, :LANES], value[:, LANES:])


def storing(out):
    def epilogue(at, real, imag):
        out[:, real_of(at)] = real
        out[:, imag_of(at)] = imag

    return epilogue


def wide_chunk(ref, at):
    return ref[:, real_of(at)], ref[:, imag_of(at)]


def refined_inverse(chunk, left, first, second, rest, epilogue, fill=(), more=()):
    n = rest.shape[0]
    count = n // LANES
    on = lax.broadcasted_iota(jnp.int32, (LANES, LANES), 0) == lax.broadcasted_iota(
        jnp.int32, (LANES, LANES), 1
    )
    eye = on.astype(F32)
    column_parts = []
    for at in range(count):
        real, imag = chunk(at)
        tiles = [jnp.where(on, part[cut(at)], 0.0) for part in (real, imag)]
        pieces = []
        for axis in (0, 1):
            dr, di = [jnp.sum(t, axis=axis, keepdims=True) for t in tiles]
            modulus = dr * dr + di * di
            pieces.append((dr / modulus, -di / modulus))
        (xr, xi), column = pieces
        column_parts.append(column)
        m_real = real * xr - imag * xi
        m_imag = real * xi + imag * xr
        m_real = jnp.concatenate(
            [m_real[cut(k)] - eye if k == at else m_real[cut(k)] for k in range(count)], axis=0
        )
        put_left(left, at, m_real, m_imag)
        put_right(first, at, m_real, m_imag)
        rest[:, real_of(at)] = -m_real
        rest[:, imag_of(at)] = -m_imag

    def square(at, real, imag):
        put_right(second, at, real, imag)
        rest[:, real_of(at)] += real
        rest[:, imag_of(at)] += imag
        rest[cut(at), real_of(at)] += eye

    product(left, first, square, fill)
    col_real, col_imag = [
        jnp.concatenate([c[part] for c in column_parts], axis=0) for part in range(2)
    ]

    def finish(at, real, imag):
        q_real = rest[:, real_of(at)] - real
        q_imag = rest[:, imag_of(at)] - imag
        epilogue(at, col_real * q_real - col_imag * q_imag, col_real * q_imag + col_imag * q_real)

    product(left, second, finish, more)


def pairs_of(refs):
    return [(refs[i], refs[i + 1]) for i in range(0, len(refs), 2)]


def parity():
    return lax.axis_index("layer") % 2


def factors(which, coupling, left, right):
    is_even = which == 0

    def fill(at):
        def run():
            real, imag = coupling[0, :, cut(at)], coupling[1, :, cut(at)]
            real_t, imag_t = coupling[0, cut(at), :].T, -coupling[1, cut(at), :].T
            put_left(left, at, jnp.where(is_even, real, real_t), jnp.where(is_even, imag, imag_t))
            put_right(
                right, at, jnp.where(is_even, real_t, real), jnp.where(is_even, imag_t, imag)
            )

        return run

    return [fill(at) for at in range(coupling.shape[-1] // LANES)]


def sandwich(which, even, left, inverse, right, half, result):
    is_even = which == 0
    product(left, inverse, lambda at, real, imag: put_left(half, at, real, imag))

    def finish(at, real, imag):
        for part, (columns, term) in enumerate(((real_of(at), real), (imag_of(at), imag))):
            result[:, columns] = jnp.where(is_even, even[part, :, cut(at)] - term, term)

    product(half, right, finish)


def first_kernel(diag, couplings, *refs):
    inverse, right, half, far_left, far_right = pairs_of(refs[:10])
    even, border, odd, near, far, sems = refs[10:16]
    left, other, first, second = pairs_of(refs[16:24])
    rest = refs[24]
    which = parity()
    count = odd.shape[-1] // LANES
    urgent = [
        pltpu.make_async_copy(diag.at[0, 1, 0, :, :, cut(at)], odd.at[:, :, cut(at)], sems.at[at])
        for at in range(count)
    ]
    later = [
        pltpu.make_async_copy(couplings.at[0, which], near, sems.at[count]),
        pltpu.make_async_copy(diag.at[0, 0, 0], even, sems.at[count + 1]),
        pltpu.make_async_copy(couplings.at[0, 1 - which], far, sems.at[count + 2]),
    ]
    for copy in urgent:
        copy.start()

    def chunk(at):
        urgent[at].wait()
        if at == count - 1:
            for copy in later:
                copy.start()
        return odd[0, :, cut(at)], odd[1, :, cut(at)]

    def after(copy, runs):
        def start():
            copy.wait()
            runs[0]()

        return [start] + runs[1:]

    refined_inverse(
        chunk,
        left,
        first,
        second,
        rest,
        lambda at, real, imag: put_right(inverse, at, real, imag),
        after(later[0], factors(which, near, other, right)),
        after(later[2], factors(1 - which, far, far_left, far_right)),
    )
    later[1].wait()
    sandwich(which, even, other, inverse, right, half, border)


def second_kernel(even, *refs):
    inverse, left, right, half = pairs_of(refs[:8])
    sandwich(1 - parity(), even, left, inverse, right, half, refs[8])


def cross_kernel(*refs):
    slow, slow_right, fast, fast_right = pairs_of(refs[:8])
    one, two = refs[8:]
    product(slow, fast_right, lambda at, real, imag: storing(one)(at, -real, -imag))
    product(fast, slow_right, lambda at, real, imag: storing(two)(at, -real, -imag))


def reduced_term(chunk, before, after, rest, epilogue, scratch):
    left, other, first, second, third = scratch
    count = before.shape[0] // LANES
    refined_inverse(
        chunk,
        left,
        first,
        second,
        rest,
        lambda at, real, imag: put_right(first, at, real, imag),
        [lambda at=at: put_left(other, at, *wide_chunk(before, at)) for at in range(count)],
        [lambda at=at: put_right(third, at, *wide_chunk(after, at)) for at in range(count)],
    )
    product(other, first, lambda at, real, imag: put_left(left, at, real, imag))
    product(left, third, epilogue)


def chip_kernel(mine, far, one, two, reduced, term, *refs):
    is_even = parity() == 0

    def chunk(at):
        parts = [
            jnp.where(is_even, b - a, a - b)
            for a, b in zip(wide_chunk(mine, at), wide_chunk(far, at))
        ]
        storing(reduced)(at, *parts)
        return parts

    reduced_term(chunk, one, two, refs[0], storing(term), pairs_of(refs[1:]))


def border_kernel(mine, far, one, two, reduced, chip_term, partial, term, *refs):
    index = lax.axis_index("layer")
    is_even = index % 2 == 0
    is_last = index == lax.axis_size("layer") - 1

    def chunk(at):
        parts = [
            jnp.where(is_even, a - b, b - a)
            for a, b in zip(wide_chunk(mine, at), wide_chunk(far, at))
        ]
        for columns, value in zip((real_of(at), imag_of(at)), parts):
            partial[:, columns] = jnp.where(
                is_even, value - chip_term[:, columns], reduced[:, columns]
            )
        return parts

    def finish(at, real, imag):
        for columns, value in ((real_of(at), real), (imag_of(at), imag)):
            value = jnp.where(is_last, 0.0, value)
            term[:, columns] = value
            partial[:, columns] -= jnp.where(is_even, 0.0, value)

    reduced_term(chunk, two, one, refs[0], finish, pairs_of(refs[1:]))


def greens_of(chunk, greens, refs):
    left, first, second = pairs_of(refs[1:])

    def finish(at, real, imag):
        greens[0, :, cut(at)] = real
        greens[1, :, cut(at)] = imag

    refined_inverse(chunk, left, first, second, refs[0], finish)


def weights_kernel(strength, transfer, offset, weights):
    for q in range(weights.shape[1]):
        mode = transfer[q]
        weight = strength[mode]
        still = offset[mode] == 0
        weights[0, q] = jnp.where(still, 2.0 * weight, 0.0)
        weights[1, q] = jnp.where(still, 0.0, weight)


def odd_greens_kernel(partial, chip_term, weights, greens, *refs):
    @pl.when(parity() == 1)
    def _():
        def chunk(at):
            return [a - b for a, b in zip(wide_chunk(partial, at), wide_chunk(chip_term, at))]

        greens_of(chunk, greens, refs)


def even_greens_kernel(partial, border_term, odd_greens, greens, *refs):
    @pl.when(parity() == 0)
    def _():
        def chunk(at):
            return [a - b for a, b in zip(wide_chunk(partial, at), wide_chunk(border_term, at))]

        greens_of(chunk, greens, refs)


def mix_kernel(phonon, weights, blocks, mixed):
    energies, momenta, depth, width = blocks.shape
    stay, move = [[weights[row, q] for q in range(momenta)] for row in range(2)]
    fold = [[phonon[e, f] for f in range(energies)] for e in range(energies)]
    for at in range(0, width, 128):
        columns = slice(at, at + 128)

        def rows_of(i, carry):
            rows = pl.ds(pl.multiple_of(i * 8, 8), 8)
            folded = []
            for k in range(momenta):
                g = [blocks[f, k, rows, columns] for f in range(energies)]
                folded.append(
                    [sum(fold[e][f] * g[f] for f in range(energies)) for e in range(energies)]
                )
            for k in range(momenta):
                moved = [
                    sum(move[q] * folded[(k - q) % momenta][e] for q in range(momenta))
                    for e in range(energies)
                ]
                for e in range(energies):
                    total = sum(stay[q] * folded[(k - q) % momenta][e] for q in range(momenta))
                    if e > 0:
                        total = total + moved[e - 1]
                    if e + 1 < energies:
                        total = total + moved[e + 1]
                    mixed[e, k, rows, columns] = total
            return carry

        lax.fori_loop(0, depth // 8, rows_of, 0)


def call(kernel, outs, operands, scratch=(), aliases=()):
    def spec(value):
        if value.ndim > 3:
            return pl.BlockSpec(memory_space=pl.ANY)
        if value.shape[-1] < LANES:
            return pl.BlockSpec(memory_space=pltpu.SMEM)
        return pl.BlockSpec(memory_space=pltpu.VMEM)

    return pl.pallas_call(
        kernel,
        out_shape=outs,
        in_specs=[spec(o) for o in operands],
        out_specs=[spec(o) for o in outs],
        scratch_shapes=list(scratch),
        input_output_aliases=dict(aliases),
        compiler_params=pltpu.CompilerParams(vmem_limit_bytes=20 * 1024 * 1024),
        cost_estimate=pl.CostEstimate(flops=COST[kernel.__name__], bytes_accessed=1, transcendentals=0),
    )(*operands)


def swap(block, axis, first):
    route = []
    for i in range(first, lax.axis_size(axis) - 1, 2):
        route += [(i, i + 1), (i + 1, i)]
    return lax.ppermute(block, axis, route)


def ahead(block, axis, first):
    return lax.ppermute(
        block, axis, [(i, i + 1) for i in range(first, lax.axis_size(axis) - 1, 2)]
    )


def body(diag_blocks, couplings, phonon_matrix, mode_strength, transfer_mode, energy_offset):
    n = diag_blocks.shape[-1]
    wide = jax.ShapeDtypeStruct((n, 2 * n), F32)
    square = jax.ShapeDtypeStruct((2, n, n), F32)
    left = [jax.ShapeDtypeStruct((n, 2 * n), BF16)] * 2
    right = [jax.ShapeDtypeStruct((2 * n, 2 * n), BF16)] * 2
    flat = [pltpu.VMEM((n, 2 * n), F32)]
    block = [pltpu.VMEM((2, n, n), F32)]
    lefts = [pltpu.VMEM((n, 2 * n), BF16)] * 2
    rights = [pltpu.VMEM((2 * n, 2 * n), BF16)] * 2

    def whole(shape):
        return pl.BlockSpec(shape, lambda i: (0,) * len(shape))

    diag_blocks, couplings = [
        pltpu.with_memory_space_constraint(v, pltpu.HBM) for v in (diag_blocks, couplings)
    ]
    *parts, even, border = call(
        first_kernel,
        right + right + left + left + right + [square, wide],
        (diag_blocks, couplings),
        block * 3 + [pltpu.SemaphoreType.DMA((n // LANES + 3,))] + lefts * 2 + rights * 2 + flat,
    )
    inverse, slow_right, slow, fast_left, fast_right = [parts[i : i + 2] for i in range(0, 10, 2)]
    border_far = swap(border, "layer", 1)
    *fast, chip = call(
        second_kernel, left + [wide], (even, *inverse, *fast_left, *fast_right)
    )
    chip, border = lax.optimization_barrier((chip, border))
    chip_far = swap(chip, "layer", 0)
    one, two = call(cross_kernel, [wide] * 2, (*slow, *slow_right, *fast, *fast_right))
    scratch = flat + lefts * 2 + rights * 3
    reduced, chip_term = call(chip_kernel, [wide] * 2, (chip, chip_far, one, two), scratch)
    from_border = ahead(chip_term, "layer", 1)
    partial, border_term = call(
        border_kernel, [wide] * 2, (border, border_far, one, two, reduced, chip_term), scratch
    )
    from_chip = ahead(border_term, "layer", 0)
    scratch = flat + lefts + rights * 2
    small = pl.BlockSpec(memory_space=pltpu.SMEM)
    transfers = jax.ShapeDtypeStruct((2,) + transfer_mode.shape, F32)
    (weights,) = call(
        weights_kernel, [transfers], (mode_strength, transfer_mode, energy_offset)
    )
    (greens,) = call(odd_greens_kernel, [square], (partial, from_chip, weights), scratch)
    (greens,) = call(
        even_greens_kernel, [square], (partial, from_border, greens), scratch, aliases={2: 0}
    )
    energies, momenta = lax.axis_size("energy"), lax.axis_size("momentum")
    group = energies * momenta
    depth = 2 * n // group
    axes = ("energy", "momentum")
    spread = lax.all_to_all(
        greens.reshape(group, depth, n), axes, split_axis=0, concat_axis=0, tiled=True
    )
    block = (energies, momenta, depth, n)
    mixed = pl.pallas_call(
        mix_kernel,
        out_shape=jax.ShapeDtypeStruct(block, F32),
        grid=(1,),
        in_specs=[small] * 2 + [whole(block)],
        out_specs=whole(block),
        compiler_params=pltpu.CompilerParams(vmem_limit_bytes=12 * 1024 * 1024),
    )(phonon_matrix, weights, spread.reshape(block))
    returned = lax.all_to_all(
        mixed.reshape(group, depth, n), axes, split_axis=0, concat_axis=0, tiled=True
    )
    return returned.reshape(1, 1, 1, 2, n, n)


COST = dict(weights_kernel=3 * 10**10, first_kernel=3 * 10**10, second_kernel=3 * 10**10, cross_kernel=3 * 10**10, chip_kernel=3 * 10**10, border_kernel=3 * 10**10, odd_greens_kernel=1, even_greens_kernel=3 * 10**10)


def solution(mesh):
    return jax.shard_map(
        body,
        mesh=mesh,
        in_specs=(
            P("momentum", "layer", "energy", None, None, None),
            P("momentum", "layer", None, None, None),
            P(),
            P(),
            P(),
            P(),
        ),
        out_specs=P("momentum", "layer", "energy", None, None, None),
        check_vma=False,
    )
```

profile of v0, /device:TPU:0, one launch (start us, length us, event | category | flops | bytes accessed | tf_op | source)
XLA Modules:
  0.0 99.0 jit_solution(7775929208482013919)
XLA Ops:
  0.0 10.6 %shard_map.65 = (bf16[768,768]{1,0:T(8,128)(2,1)S(1)}, bf16[768,768]{1,0:T(8,128)(2,1)S(1)}, bf16[768,768]{1,0:T(8,128)(2,1)S(1)}, bf16[768,768]{1,0:T(8,128)(2,...) custom-call(f32[1,2,1,2,384,384]{5,4,3,2,1,0:T(8,128)} %diag.1, ...), custom_call_target="tpu_custom_call" | custom-call | flops 30000001024 | bytes 1 | tf_op jit(solution)/shard_map/pallas_call | solution.py:355
  10.6 0.7 collective-permute-start
  11.4 3.7 %shard_map.66 = (bf16[384,768]{1,0:T(8,128)(2,1)S(1)}, bf16[384,768]{1,0:T(8,128)(2,1)S(1)}, f32[384,768]{1,0:T(8,128)S(1)}) custom-call(f32[2,384,384]{2,1,0:T(8,128)S(1)} %get-tuple-element.28.even, bf16[768,768]{1,0:T(8,128)(2,1)S(1)} %get-tuple-element.29.refs_0_, bf16[768,768]{1,0:T(8,128)(2,1)S(1)} %get-tuple-element.30.refs_1_, ...), custom_call_target="tpu_custom_call" | custom-call | flops 30000001024 | bytes 1 | tf_op jit(solution)/shard_map/pallas_call | solution.py:355
  15.1 3.5 %collective-permute-start.1 = (f32[384,768]{1,0:T(8,128)S(1)}, f32[384,768]{1,0:T(8,128)S(1)}, u32[]{:S(2)}, u32[]{:S(2)}) collective-permute-start(f32[384,768]{1,0:T(8,128)S(1)} %get-tuple-element.46.mine), channel_id=1, source_target_pairs={{0,16},{16,0},{32,48},{48,32},{64,80},{80,64},{96,112},{112,96},{1... | collective-permute-start | bytes 3538952 | tf_op jit(solution)/shard_map/ppermute | solution.py:371
  18.6 2.9 %shard_map.67 = (f32[384,768]{1,0:T(8,128)S(1)}, f32[384,768]{1,0:T(8,128)S(1)}) custom-call(bf16[384,768]{1,0:T(8,128)(2,1)S(1)} %get-tuple-element.38.refs_0_, bf16[384,768]{1,0:T(8,128)(2,1)S(1)} %get-tuple-element.39.refs_1_, bf16[768,768]{1,0:T(8,128)(2,1)S(1)} %get-tuple-element.40.refs_2_, bf16[768,768]{1,0:T(8,128)(2,1)S(1)} %get-tuple-element.41.refs_3_, ...), custom_call_target="tpu_custom_call" | custom-call | flops 30000001024 | bytes 1 | tf_op jit(solution)/shard_map/pallas_call | solution.py:355
  21.5 0.0 collective-permute-done.1.far
  21.6 7.4 %shard_map.68 = (f32[384,768]{1,0:T(8,128)S(1)}, f32[384,768]{1,0:T(8,128)S(1)}) custom-call(f32[384,768]{1,0:T(8,128)S(1)} %get-tuple-element.46.mine, f32[384,768]{1,0:T(8,128)S(1)} %collective-permute-done.1.far, f32[384,768]{1,0:T(8,128)S(1)} %get-tuple-element.44.one, f32[384,768]{1,0:T(8,128)S(1)} %get-tuple-element.45.two), custom_call_target="tpu_custom_call" | custom-call | flops 30000001024 | bytes 1 | tf_op jit(solution)/shard_map/pallas_call | solution.py:355
  29.0 1.0 collective-permute-start.2
  29.9 0.0 collective-permute-done.far
  29.9 0.0 copy-start.1
  29.9 0.0 copy-start.2
  30.0 0.0 copy-start.3
  30.0 7.4 %shard_map.69 = (f32[384,768]{1,0:T(8,128)S(1)}, f32[384,768]{1,0:T(8,128)S(1)}) custom-call(f32[384,768]{1,0:T(8,128)S(1)} %get-tuple-element.37.mine, f32[384,768]{1,0:T(8,128)S(1)} %collective-permute-done.far, f32[384,768]{1,0:T(8,128)S(1)} %get-tuple-element.44.one, f32[384,768]{1,0:T(8,128)S(1)} %get-tuple-element.45.two, ...), custom_call_target="tpu_custom_call" | custom-call | flops 30000001024 | bytes 1 | tf_op jit(solution)/shard_map/pallas_call | solution.py:355
  37.4 5.3 %collective-permute-start.3 = (f32[384,768]{1,0:T(8,128)S(1)}, f32[384,768]{1,0:T(8,128)S(1)}, u32[]{:S(2)}, u32[]{:S(2)}) collective-permute-start(f32[384,768]{1,0:T(8,128)S(1)} %get-tuple-element.50), channel_id=1, source_target_pairs={{0,16},{32,48},{64,80},{96,112},{1,17},{33,49},{65,81},{97,113},{2... | collective-permute-start | bytes 3538952 | tf_op jit(solution)/shard_map/ppermute | solution.py:375
  42.7 0.0 copy-done.1
  42.7 0.0 copy-done.2
  42.7 0.0 copy-done.3
  42.7 1.2 %shard_map.64.weights = f32[2,4]{1,0:T(2,128)S(1)} custom-call(f32[3]{0:T(128)S(1)} %copy-done.1, s32[4]{0:T(128)S(1)} %copy-done.2, s32[3]{0:T(128)S(1)} %copy-done.3), custom_call_target="tpu_custom_call" | custom-call | flops 30000001024 | bytes 1 | tf_op jit(solution)/shard_map/pallas_call | solution.py:355
  43.9 1.2 %collective-permute-done.3.chip_term = f32[384,768]{1,0:T(8,128)S(1)} collective-permute-done((f32[384,768]{1,0:T(8,128)S(1)}, f32[384,768]{1,0:T(8,128)S(1)}, u32[]{:S(2)}, u32[]{:S(2)}) %collective-permute-start.3) | collective-permute-done | bytes 1179680 | tf_op jit(solution)/shard_map/ppermute | solution.py:375
  45.1 0.6 shard_map.70.odd_greens
  45.6 0.0 collective-permute-done.2.border_term
  45.6 3.6 %shard_map.71 = f32[2,384,384]{2,1,0:T(8,128)S(1)} custom-call(f32[384,768]{1,0:T(8,128)S(1)} %get-tuple-element.49.partial, f32[384,768]{1,0:T(8,128)S(1)} %collective-permute-done.2.border_term, f32[2,384,384]{2,1,0:T(8,128)S(1)} %shard_map.70.odd_greens), custom_call_target="tpu_custom_call", output_to_operand_aliasing={{}: (2, {})} | custom-call | flops 30000001024 | bytes 1 | tf_op jit(solution)/shard_map/pallas_call | solution.py:355
  49.2 0.0 copy-start
  49.2 26.0 %all_to_all.10 = f32[16,48,384]{2,1,0:T(8,128)S(1)} all-to-all(f32[16,48,384]{2,1,0:T(8,128)S(1)} %bitcast.6), channel_id=1, replica_groups=mesh['layer'=8,'energy'=4,'momentum'=4] {'energy','momentum'}, dimensions={0} | all-to-all | bytes 2359296 | tf_op jit(solution)/shard_map/all_to_all | solution.py:432
  75.2 0.0 copy-done
  75.2 1.6 %shard_map.72 = f32[4,4,48,384]{3,2,1,0:T(8,128)S(1)} custom-call(f32[4,4]{1,0:T(4,128)S(1)} %copy-done, f32[2,4]{1,0:T(2,128)S(1)} %shard_map.64.weights, f32[4,4,48,384]{3,2,1,0:T(8,128)S(1)} %bitcast.4), custom_call_target="tpu_custom_call" | custom-call | tf_op jit(solution)/shard_map/pallas_call | solution.py:436
  76.8 21.2 %all_to_all.11 = f32[16,48,384]{2,1,0:T(8,128)S(1)} all-to-all(f32[16,48,384]{2,1,0:T(8,128)S(1)} %bitcast.5), channel_id=1, replica_groups=mesh['layer'=8,'energy'=4,'momentum'=4] {'energy','momentum'}, dimensions={0} | all-to-all | bytes 2359296 | tf_op jit(solution)/shard_map/all_to_all | solution.py:444
  98.0 1.0 %copy.10 = f32[1,1,1,2,384,384]{5,4,3,2,1,0:T(8,128)} copy(f32[1,1,1,2,384,384]{5,4,3,2,1,0:T(8,128)S(1)} %bitcast.7) | data formatting | bytes 2359296
Async XLA Ops:
  10.6 19.3 %collective-permute-start = (f32[384,768]{1,0:T(8,128)S(1)}, f32[384,768]{1,0:T(8,128)S(1)}, u32[]{:S(2)}, u32[]{:S(2)}) collective-permute-start(f32[384,768]{1,0:T(8,128)S(1)} %get-tuple-element.37.mine), channel_id=1, source_target_pairs={{16,32},{32,16},{48,64},{64,48},{80,96},{96,80},{17,33},{33,17},{4... | collective-permute-start | bytes 3538952 | tf_op jit(solution)/shard_map/ppermute | solution.py:371
  15.1 6.5 %collective-permute-start.1 = (f32[384,768]{1,0:T(8,128)S(1)}, f32[384,768]{1,0:T(8,128)S(1)}, u32[]{:S(2)}, u32[]{:S(2)}) collective-permute-start(f32[384,768]{1,0:T(8,128)S(1)} %get-tuple-element.46.mine), channel_id=1, source_target_pairs={{0,16},{16,0},{32,48},{48,32},{64,80},{80,64},{96,112},{112,96},{1... | collective-permute-start | bytes 3538952 | tf_op jit(solution)/shard_map/ppermute | solution.py:371
  29.0 16.7 %collective-permute-start.2 = (f32[384,768]{1,0:T(8,128)S(1)}, f32[384,768]{1,0:T(8,128)S(1)}, u32[]{:S(2)}, u32[]{:S(2)}) collective-permute-start(f32[384,768]{1,0:T(8,128)S(1)} %get-tuple-element.48.chip_term), channel_id=1, source_target_pairs={{16,32},{48,64},{80,96},{17,33},{49,65},{81,97},{18,34},{50,66},{8... | collective-permute-start | bytes 3538952 | tf_op jit(solution)/shard_map/ppermute | solution.py:375
  29.9 12.8 %copy-start.1 = (f32[3]{0:T(128)S(1)}, f32[3]{0:T(128)}, u32[]{:S(2)}) copy-start(f32[3]{0:T(128)} %strength.1) | copy-start | bytes 40
  29.9 12.8 %copy-start.2 = (s32[4]{0:T(128)S(1)}, s32[4]{0:T(128)}, u32[]{:S(2)}) copy-start(s32[4]{0:T(128)} %transfer.1) | copy-start | bytes 52
  30.0 12.7 %copy-start.3 = (s32[3]{0:T(128)S(1)}, s32[3]{0:T(128)}, u32[]{:S(2)}) copy-start(s32[3]{0:T(128)} %offset.1) | copy-start | bytes 40
  37.4 7.6 %collective-permute-start.3 = (f32[384,768]{1,0:T(8,128)S(1)}, f32[384,768]{1,0:T(8,128)S(1)}, u32[]{:S(2)}, u32[]{:S(2)}) collective-permute-start(f32[384,768]{1,0:T(8,128)S(1)} %get-tuple-element.50), channel_id=1, source_target_pairs={{0,16},{32,48},{64,80},{96,112},{1,17},{33,49},{65,81},{97,113},{2... | collective-permute-start | bytes 3538952 | tf_op jit(solution)/shard_map/ppermute | solution.py:375
  49.2 26.0 %copy-start = (f32[4,4]{1,0:T(4,128)S(1)}, f32[4,4]{1,0:T(4,128)}, u32[]{:S(2)}) copy-start(f32[4,4]{1,0:T(4,128)} %phonon.1) | copy-start | bytes 196
where the time goes:
time: 99.3 us; the launch traced here: 99 us
  blocking collectives  47.2 us (48%)
  Pallas kernels  38.9 us (39%)
  starting transfers between devices  10.5 us (11%)
  waiting for transfers between devices  1.19 us (1%)
  local copies, waits for them, and re-layouts  1.04 us (1%)
    pallas_call x8, Pallas kernels, call(): pl.pallas_call(kernel, out_shape=outs, in_specs=[spec(o) for o in operand...  37.4 us
    all_to_all x1, blocking collectives, body(): lax.all_to_all(greens.reshape(group, depth, n), axes, split_axis=0, conca...  26 us
    all_to_all x1, blocking collectives, body(): lax.all_to_all(mixed.reshape(group, depth, n), axes, split_axis=0, concat...  21.2 us
    ppermute x2, starting transfers between devices, ahead(): lax.ppermute(block, axis, [(i, i + 1) for i in range(first, lax.axis_size...  6.22 us
    ppermute x2, starting transfers between devices, swap(): return lax.ppermute(block, axis, route)  4.28 us
  transfers between devices with their start and end apart: 4, of which 1 were waited for; matrix products, arithmetic and copies ran while one was open for 0% of the time, Pallas kernels for 23%

commit v1 on v0

--- a/solution.py
+++ b/solution.py
@@ -55,11 +55,11 @@
         columns = pair(at)
         high = right[0][:, columns]
         lh = left[0][...]
-        value = (
-            jnp.dot(lh, high, preferred_element_type=F32)
-            + jnp.dot(lh, right[1][:, columns], preferred_element_type=F32)
-            + jnp.dot(left[1][...], high, preferred_element_type=F32)
-        )
+        value = jnp.dot(lh, high, preferred_element_type=F32)
+        for low in right[1:]:
+            value += jnp.dot(lh, low[:, columns], preferred_element_type=F32)
+        for low in left[1:]:
+            value += jnp.dot(low[...], high, preferred_element_type=F32)
         if at < len(fill):
             fill[at]()
         epilogue(at, value[:, :LANES], value[:, LANES:])
@@ -168,22 +168,26 @@
     which = parity()
     count = odd.shape[-1] // LANES
     urgent = [
-        pltpu.make_async_copy(diag.at[0, 1, 0, :, :, cut(at)], odd.at[:, :, cut(at)], sems.at[at])
+        pltpu.make_async_copy(
+            diag.at[0, 1, 0, part, cut(at)], odd.at[part, cut(at)], sems.at[part * count + at]
+        )
+        for part in range(2)
         for at in range(count)
     ]
     later = [
-        pltpu.make_async_copy(couplings.at[0, which], near, sems.at[count]),
-        pltpu.make_async_copy(diag.at[0, 0, 0], even, sems.at[count + 1]),
-        pltpu.make_async_copy(couplings.at[0, 1 - which], far, sems.at[count + 2]),
+        pltpu.make_async_copy(couplings.at[0, which], near, sems.at[2 * count]),
+        pltpu.make_async_copy(diag.at[0, 0, 0], even, sems.at[2 * count + 1]),
+        pltpu.make_async_copy(couplings.at[0, 1 - which], far, sems.at[2 * count + 2]),
     ]
     for copy in urgent:
         copy.start()
 
+    for copy in urgent:
+        copy.wait()
+    for copy in later:
+        copy.start()
+
     def chunk(at):
-        urgent[at].wait()
-        if at == count - 1:
-            for copy in later:
-                copy.start()
         return odd[0, :, cut(at)], odd[1, :, cut(at)]
 
     def after(copy, runs):
@@ -195,9 +199,9 @@
 
     refined_inverse(
         chunk,
-        left,
-        first,
-        second,
+        left[:1],
+        first[:1],
+        second[:1],
         rest,
         lambda at, real, imag: put_right(inverse, at, real, imag),
         after(later[0], factors(which, near, other, right)),
@@ -224,9 +228,9 @@
     count = before.shape[0] // LANES
     refined_inverse(
         chunk,
-        left,
-        first,
-        second,
+        left[:1],
+        first[:1],
+        second[:1],
         rest,
         lambda at, real, imag: put_right(first, at, real, imag),
         [lambda at=at: put_left(other, at, *wide_chunk(before, at)) for at in range(count)],
@@ -398,7 +402,7 @@
         first_kernel,
         right + right + left + left + right + [square, wide],
         (diag_blocks, couplings),
-        block * 3 + [pltpu.SemaphoreType.DMA((n // LANES + 3,))] + lefts * 2 + rights * 2 + flat,
+        block * 3 + [pltpu.SemaphoreType.DMA((2 * (n // LANES) + 3,))] + lefts * 2 + rights * 2 + flat,
     )
     inverse, slow_right, slow, fast_left, fast_right = [parts[i : i + 2] for i in range(0, 10, 2)]
     border_far = swap(border, "layer", 1)

time: 99.3 us -> 93.2 us (0.939)
  Pallas kernels: 38.9 us -> 33.1 us
    pallas_call x8, Pallas kernels: 37.4 us -> 31.5 us  [call(): pl.pallas_call(kernel, out_shape=outs, in_specs=[spec(o) for o in operand...]
  transfers between devices with their start and end apart: 4 -> 4, of which waited for: 1 -> 1; matrix products, arithmetic and copies ran while one was open for 0% -> 0% of each run, Pallas kernels for 23% -> 21%
where the time goes in v1:
time: 93.2 us; the launch traced here: 93 us
  blocking collectives  47.2 us (51%)
  Pallas kernels  33.1 us (36%)
  starting transfers between devices  10.3 us (11%)
  waiting for transfers between devices  1.19 us (1%)
  local copies, waits for them, and re-layouts  1.04 us (1%)
    pallas_call x8, Pallas kernels, call(): pl.pallas_call(kernel, out_shape=outs, in_specs=[spec(o) for o in operand...  31.5 us
    all_to_all x1, blocking collectives, body(): lax.all_to_all(greens.reshape(group, depth, n), axes, split_axis=0, conca...  26 us
    all_to_all x1, blocking collectives, body(): lax.all_to_all(mixed.reshape(group, depth, n), axes, split_axis=0, concat...  21.2 us
    ppermute x2, starting transfers between devices, ahead(): lax.ppermute(block, axis, [(i, i + 1) for i in range(first, lax.axis_size...  5.99 us
    ppermute x2, starting transfers between devices, swap(): return lax.ppermute(block, axis, route)  4.28 us
  transfers between devices with their start and end apart: 4, of which 1 were waited for; matrix products, arithmetic and copies ran while one was open for 0% of the time, Pallas kernels for 21%

profile of v1, /device:TPU:0, one launch (start us, length us, event | category | flops | bytes accessed | tf_op | source)
XLA Modules:
  0.0 93.0 jit_solution(5610212103898816911)
XLA Ops:
  0.0 8.7 %shard_map.65 = (bf16[768,768]{1,0:T(8,128)(2,1)S(1)}, bf16[768,768]{1,0:T(8,128)(2,1)S(1)}, bf16[768,768]{1,0:T(8,128)(2,1)S(1)}, bf16[768,768]{1,0:T(8,128)(2,...) custom-call(f32[1,2,1,2,384,384]{5,4,3,2,1,0:T(8,128)} %diag.1, ...), custom_call_target="tpu_custom_call" | custom-call | flops 30000001024 | bytes 1 | tf_op jit(solution)/shard_map/pallas_call | solution.py:359
  8.7 0.7 collective-permute-start
  9.5 3.7 %shard_map.66 = (bf16[384,768]{1,0:T(8,128)(2,1)S(1)}, bf16[384,768]{1,0:T(8,128)(2,1)S(1)}, f32[384,768]{1,0:T(8,128)S(1)}) custom-call(f32[2,384,384]{2,1,0:T(8,128)S(1)} %get-tuple-element.28.even, bf16[768,768]{1,0:T(8,128)(2,1)S(1)} %get-tuple-element.29.refs_0_, bf16[768,768]{1,0:T(8,128)(2,1)S(1)} %get-tuple-element.30.refs_1_, ...), custom_call_target="tpu_custom_call" | custom-call | flops 30000001024 | bytes 1 | tf_op jit(solution)/shard_map/pallas_call | solution.py:359
  13.2 3.5 %collective-permute-start.1 = (f32[384,768]{1,0:T(8,128)S(1)}, f32[384,768]{1,0:T(8,128)S(1)}, u32[]{:S(2)}, u32[]{:S(2)}) collective-permute-start(f32[384,768]{1,0:T(8,128)S(1)} %get-tuple-element.46.mine), channel_id=1, source_target_pairs={{0,16},{16,0},{32,48},{48,32},{64,80},{80,64},{96,112},{112,96},{1... | collective-permute-start | bytes 3538952 | tf_op jit(solution)/shard_map/ppermute | solution.py:375
  16.7 2.9 %shard_map.67 = (f32[384,768]{1,0:T(8,128)S(1)}, f32[384,768]{1,0:T(8,128)S(1)}) custom-call(bf16[384,768]{1,0:T(8,128)(2,1)S(1)} %get-tuple-element.38.refs_0_, bf16[384,768]{1,0:T(8,128)(2,1)S(1)} %get-tuple-element.39.refs_1_, bf16[768,768]{1,0:T(8,128)(2,1)S(1)} %get-tuple-element.40.refs_2_, bf16[768,768]{1,0:T(8,128)(2,1)S(1)} %get-tuple-element.41.refs_3_, ...), custom_call_target="tpu_custom_call" | custom-call | flops 30000001024 | bytes 1 | tf_op jit(solution)/shard_map/pallas_call | solution.py:359
  19.6 0.0 collective-permute-done.1.far
  19.7 5.3 %shard_map.68 = (f32[384,768]{1,0:T(8,128)S(1)}, f32[384,768]{1,0:T(8,128)S(1)}) custom-call(f32[384,768]{1,0:T(8,128)S(1)} %get-tuple-element.46.mine, f32[384,768]{1,0:T(8,128)S(1)} %collective-permute-done.1.far, f32[384,768]{1,0:T(8,128)S(1)} %get-tuple-element.44.one, f32[384,768]{1,0:T(8,128)S(1)} %get-tuple-element.45.two), custom_call_target="tpu_custom_call" | custom-call | flops 30000001024 | bytes 1 | tf_op jit(solution)/shard_map/pallas_call | solution.py:359
  25.0 0.7 collective-permute-start.2
  25.7 0.0 collective-permute-done.far
  25.7 0.0 copy-start.1
  25.7 0.0 copy-start.2
  25.8 0.0 copy-start.3
  25.8 5.4 %shard_map.69 = (f32[384,768]{1,0:T(8,128)S(1)}, f32[384,768]{1,0:T(8,128)S(1)}) custom-call(f32[384,768]{1,0:T(8,128)S(1)} %get-tuple-element.37.mine, f32[384,768]{1,0:T(8,128)S(1)} %collective-permute-done.far, f32[384,768]{1,0:T(8,128)S(1)} %get-tuple-element.44.one, f32[384,768]{1,0:T(8,128)S(1)} %get-tuple-element.45.two, ...), custom_call_target="tpu_custom_call" | custom-call | flops 30000001024 | bytes 1 | tf_op jit(solution)/shard_map/pallas_call | solution.py:359
  31.1 5.3 %collective-permute-start.3 = (f32[384,768]{1,0:T(8,128)S(1)}, f32[384,768]{1,0:T(8,128)S(1)}, u32[]{:S(2)}, u32[]{:S(2)}) collective-permute-start(f32[384,768]{1,0:T(8,128)S(1)} %get-tuple-element.50), channel_id=1, source_target_pairs={{0,16},{32,48},{64,80},{96,112},{1,17},{33,49},{65,81},{97,113},{2... | collective-permute-start | bytes 3538952 | tf_op jit(solution)/shard_map/ppermute | solution.py:379
  36.4 0.0 copy-done.1
  36.4 0.0 copy-done.2
  36.4 0.0 copy-done.3
  36.4 1.2 %shard_map.64.weights = f32[2,4]{1,0:T(2,128)S(1)} custom-call(f32[3]{0:T(128)S(1)} %copy-done.1, s32[4]{0:T(128)S(1)} %copy-done.2, s32[3]{0:T(128)S(1)} %copy-done.3), custom_call_target="tpu_custom_call" | custom-call | flops 30000001024 | bytes 1 | tf_op jit(solution)/shard_map/pallas_call | solution.py:359
  37.6 1.2 %collective-permute-done.3.chip_term = f32[384,768]{1,0:T(8,128)S(1)} collective-permute-done((f32[384,768]{1,0:T(8,128)S(1)}, f32[384,768]{1,0:T(8,128)S(1)}, u32[]{:S(2)}, u32[]{:S(2)}) %collective-permute-start.3) | collective-permute-done | bytes 1179680 | tf_op jit(solution)/shard_map/ppermute | solution.py:379
  38.8 0.8 shard_map.70.odd_greens
  39.6 0.0 collective-permute-done.2.border_term
  39.6 3.6 %shard_map.71 = f32[2,384,384]{2,1,0:T(8,128)S(1)} custom-call(f32[384,768]{1,0:T(8,128)S(1)} %get-tuple-element.49.partial, f32[384,768]{1,0:T(8,128)S(1)} %collective-permute-done.2.border_term, f32[2,384,384]{2,1,0:T(8,128)S(1)} %shard_map.70.odd_greens), custom_call_target="tpu_custom_call", output_to_operand_aliasing={{}: (2, {})} | custom-call | flops 30000001024 | bytes 1 | tf_op jit(solution)/shard_map/pallas_call | solution.py:359
  43.2 0.0 copy-start
  43.2 26.0 %all_to_all.10 = f32[16,48,384]{2,1,0:T(8,128)S(1)} all-to-all(f32[16,48,384]{2,1,0:T(8,128)S(1)} %bitcast.6), channel_id=1, replica_groups=mesh['layer'=8,'energy'=4,'momentum'=4] {'energy','momentum'}, dimensions={0} | all-to-all | bytes 2359296 | tf_op jit(solution)/shard_map/all_to_all | solution.py:436
  69.2 0.0 copy-done
  69.2 1.6 %shard_map.72 = f32[4,4,48,384]{3,2,1,0:T(8,128)S(1)} custom-call(f32[4,4]{1,0:T(4,128)S(1)} %copy-done, f32[2,4]{1,0:T(2,128)S(1)} %shard_map.64.weights, f32[4,4,48,384]{3,2,1,0:T(8,128)S(1)} %bitcast.4), custom_call_target="tpu_custom_call" | custom-call | tf_op jit(solution)/shard_map/pallas_call | solution.py:440
  70.8 21.2 %all_to_all.11 = f32[16,48,384]{2,1,0:T(8,128)S(1)} all-to-all(f32[16,48,384]{2,1,0:T(8,128)S(1)} %bitcast.5), channel_id=1, replica_groups=mesh['layer'=8,'energy'=4,'momentum'=4] {'energy','momentum'}, dimensions={0} | all-to-all | bytes 2359296 | tf_op jit(solution)/shard_map/all_to_all | solution.py:448
  92.0 1.0 %copy.10 = f32[1,1,1,2,384,384]{5,4,3,2,1,0:T(8,128)} copy(f32[1,1,1,2,384,384]{5,4,3,2,1,0:T(8,128)S(1)} %bitcast.7) | data formatting | bytes 2359296
Async XLA Ops:
  8.7 17.0 %collective-permute-start = (f32[384,768]{1,0:T(8,128)S(1)}, f32[384,768]{1,0:T(8,128)S(1)}, u32[]{:S(2)}, u32[]{:S(2)}) collective-permute-start(f32[384,768]{1,0:T(8,128)S(1)} %get-tuple-element.37.mine), channel_id=1, source_target_pairs={{16,32},{32,16},{48,64},{64,48},{80,96},{96,80},{17,33},{33,17},{4... | collective-permute-start | bytes 3538952 | tf_op jit(solution)/shard_map/ppermute | solution.py:375
  13.2 6.5 %collective-permute-start.1 = (f32[384,768]{1,0:T(8,128)S(1)}, f32[384,768]{1,0:T(8,128)S(1)}, u32[]{:S(2)}, u32[]{:S(2)}) collective-permute-start(f32[384,768]{1,0:T(8,128)S(1)} %get-tuple-element.46.mine), channel_id=1, source_target_pairs={{0,16},{16,0},{32,48},{48,32},{64,80},{80,64},{96,112},{112,96},{1... | collective-permute-start | bytes 3538952 | tf_op jit(solution)/shard_map/ppermute | solution.py:375
  25.0 14.6 %collective-permute-start.2 = (f32[384,768]{1,0:T(8,128)S(1)}, f32[384,768]{1,0:T(8,128)S(1)}, u32[]{:S(2)}, u32[]{:S(2)}) collective-permute-start(f32[384,768]{1,0:T(8,128)S(1)} %get-tuple-element.48.chip_term), channel_id=1, source_target_pairs={{16,32},{48,64},{80,96},{17,33},{49,65},{81,97},{18,34},{50,66},{8... | collective-permute-start | bytes 3538952 | tf_op jit(solution)/shard_map/ppermute | solution.py:379
  25.7 10.7 %copy-start.1 = (f32[3]{0:T(128)S(1)}, f32[3]{0:T(128)}, u32[]{:S(2)}) copy-start(f32[3]{0:T(128)} %strength.1) | copy-start | bytes 40
  25.7 10.7 %copy-start.2 = (s32[4]{0:T(128)S(1)}, s32[4]{0:T(128)}, u32[]{:S(2)}) copy-start(s32[4]{0:T(128)} %transfer.1) | copy-start | bytes 52
  25.8 10.7 %copy-start.3 = (s32[3]{0:T(128)S(1)}, s32[3]{0:T(128)}, u32[]{:S(2)}) copy-start(s32[3]{0:T(128)} %offset.1) | copy-start | bytes 40
  31.1 7.6 %collective-permute-start.3 = (f32[384,768]{1,0:T(8,128)S(1)}, f32[384,768]{1,0:T(8,128)S(1)}, u32[]{:S(2)}, u32[]{:S(2)}) collective-permute-start(f32[384,768]{1,0:T(8,128)S(1)} %get-tuple-element.50), channel_id=1, source_target_pairs={{0,16},{32,48},{64,80},{96,112},{1,17},{33,49},{65,81},{97,113},{2... | collective-permute-start | bytes 3538952 | tf_op jit(solution)/shard_map/ppermute | solution.py:379
  43.2 26.0 %copy-start = (f32[4,4]{1,0:T(4,128)S(1)}, f32[4,4]{1,0:T(4,128)}, u32[]{:S(2)}) copy-start(f32[4,4]{1,0:T(4,128)} %phonon.1) | copy-start | bytes 196

commit v2 on v1

--- a/solution.py
+++ b/solution.py
@@ -149,9 +149,9 @@
     return [fill(at) for at in range(coupling.shape[-1] // LANES)]
 
 
-def sandwich(which, even, left, inverse, right, half, result):
+def sandwich(which, even, left, inverse, right, half, result, fill=()):
     is_even = which == 0
-    product(left, inverse, lambda at, real, imag: put_left(half, at, real, imag))
+    product(left, inverse, lambda at, real, imag: put_left(half, at, real, imag), fill)
 
     def finish(at, real, imag):
         for part, (columns, term) in enumerate(((real_of(at), real), (imag_of(at), imag))):
@@ -197,6 +197,7 @@
 
         return [start] + runs[1:]
 
+    near_fill = factors(which, near, other, right)
     refined_inverse(
         chunk,
         left[:1],
@@ -204,11 +205,12 @@
         second[:1],
         rest,
         lambda at, real, imag: put_right(inverse, at, real, imag),
-        after(later[0], factors(which, near, other, right)),
-        after(later[2], factors(1 - which, far, far_left, far_right)),
+        [lambda: None, after(later[0], near_fill[:1])[0], near_fill[1]],
+        near_fill[2:],
     )
     later[1].wait()
-    sandwich(which, even, other, inverse, right, half, border)
+    fill = after(later[2], factors(1 - which, far, far_left, far_right))
+    sandwich(which, even, other, inverse, right, half, border, fill)
 
 
 def second_kernel(even, *refs):
@@ -289,13 +291,21 @@
     refined_inverse(chunk, left, first, second, refs[0], finish)
 
 
-def weights_kernel(strength, transfer, offset, weights):
-    for q in range(weights.shape[1]):
+def weights_kernel(phonon, strength, transfer, offset, weights):
+    energies, transfers = phonon.shape[0], transfer.shape[0]
+
+    def put(row, value):
+        weights[row : row + 1, :] = jnp.full((1, LANES), value, F32)
+
+    for e in range(energies):
+        for f in range(energies):
+            put(e * energies + f, phonon[e, f])
+    for q in range(transfers):
         mode = transfer[q]
         weight = strength[mode]
         still = offset[mode] == 0
-        weights[0, q] = jnp.where(still, 2.0 * weight, 0.0)
-        weights[1, q] = jnp.where(still, 0.0, weight)
+        put(energies * energies + q, jnp.where(still, 2.0 * weight, 0.0))
+        put(energies * energies + transfers + q, jnp.where(still, 0.0, weight))
 
 
 def odd_greens_kernel(partial, chip_term, weights, greens, *refs):
@@ -316,10 +326,11 @@
         greens_of(chunk, greens, refs)
 
 
-def mix_kernel(phonon, weights, blocks, mixed):
+def mix_kernel(weights, blocks, mixed):
     energies, momenta, depth, width = blocks.shape
-    stay, move = [[weights[row, q] for q in range(momenta)] for row in range(2)]
-    fold = [[phonon[e, f] for f in range(energies)] for e in range(energies)]
+    rows = [weights[row : row + 1, :] for row in range(energies * energies + 2 * momenta)]
+    fold = [rows[e * energies : (e + 1) * energies] for e in range(energies)]
+    stay, move = rows[-2 * momenta : -momenta], rows[-momenta:]
     for at in range(0, width, 128):
         columns = slice(at, at + 128)
 
@@ -345,7 +356,7 @@
                     mixed[e, k, rows, columns] = total
             return carry
 
-        lax.fori_loop(0, depth // 8, rows_of, 0)
+        lax.fori_loop(0, depth // 8, rows_of, 0, unroll=2)
 
 
 def call(kernel, outs, operands, scratch=(), aliases=()):
@@ -392,9 +403,6 @@
     lefts = [pltpu.VMEM((n, 2 * n), BF16)] * 2
     rights = [pltpu.VMEM((2 * n, 2 * n), BF16)] * 2
 
-    def whole(shape):
-        return pl.BlockSpec(shape, lambda i: (0,) * len(shape))
-
     diag_blocks, couplings = [
         pltpu.with_memory_space_constraint(v, pltpu.HBM) for v in (diag_blocks, couplings)
     ]
@@ -419,17 +427,16 @@
         border_kernel, [wide] * 2, (border, border_far, one, two, reduced, chip_term), scratch
     )
     from_chip = ahead(border_term, "layer", 0)
+    energies, momenta = lax.axis_size("energy"), lax.axis_size("momentum")
+    table = jax.ShapeDtypeStruct((energies * energies + 2 * momenta, LANES), F32)
+    (weights,) = call(
+        weights_kernel, [table], (phonon_matrix, mode_strength, transfer_mode, energy_offset)
+    )
     scratch = flat + lefts + rights * 2
-    small = pl.BlockSpec(memory_space=pltpu.SMEM)
-    transfers = jax.ShapeDtypeStruct((2,) + transfer_mode.shape, F32)
-    (weights,) = call(
-        weights_kernel, [transfers], (mode_strength, transfer_mode, energy_offset)
-    )
     (greens,) = call(odd_greens_kernel, [square], (partial, from_chip, weights), scratch)
     (greens,) = call(
         even_greens_kernel, [square], (partial, from_border, greens), scratch, aliases={2: 0}
     )
-    energies, momenta = lax.axis_size("energy"), lax.axis_size("momentum")
     group = energies * momenta
     depth = 2 * n // group
     axes = ("energy", "momentum")
@@ -440,11 +447,10 @@
     mixed = pl.pallas_call(
         mix_kernel,
         out_shape=jax.ShapeDtypeStruct(block, F32),
-        grid=(1,),
-        in_specs=[small] * 2 + [whole(block)],
-        out_specs=whole(block),
+        in_specs=[pl.BlockSpec(memory_space=pltpu.VMEM)] * 2,
+        out_specs=pl.BlockSpec(memory_space=pltpu.VMEM),
         compiler_params=pltpu.CompilerParams(vmem_limit_bytes=12 * 1024 * 1024),
-    )(phonon_matrix, weights, spread.reshape(block))
+    )(weights, spread.reshape(block))
     returned = lax.all_to_all(
         mixed.reshape(group, depth, n), axes, split_axis=0, concat_axis=0, tiled=True
     )

time: 93.2 us -> 91.5 us (0.982)
  Pallas kernels: 33.1 us -> 30.7 us
    pallas_call x8, Pallas kernels: 31.5 us -> 29.8 us  [call(): pl.pallas_call(kernel, out_shape=outs, in_specs=[spec(o) for o in operand...]
  transfers between devices with their start and end apart: 4 -> 4, of which waited for: 1 -> 1; matrix products, arithmetic and copies ran while one was open for 0% -> 0% of each run, Pallas kernels for 21% -> 20%
where the time goes in v2:
time: 91.5 us; the launch traced here: 91.2 us
  blocking collectives  47.3 us (52%)
  Pallas kernels  30.7 us (34%)
  starting transfers between devices  10.3 us (11%)
  waiting for transfers between devices  1.74 us (2%)
  local copies, waits for them, and re-layouts  1.04 us (1%)
    pallas_call x8, Pallas kernels, call(): pl.pallas_call(kernel, out_shape=outs, in_specs=[spec(o) for o in operand...  29.8 us
    all_to_all x1, blocking collectives, body(): lax.all_to_all(greens.reshape(group, depth, n), axes, split_axis=0, conca...  26 us
    all_to_all x1, blocking collectives, body(): lax.all_to_all(mixed.reshape(group, depth, n), axes, split_axis=0, concat...  21.2 us
    ppermute x2, starting transfers between devices, ahead(): lax.ppermute(block, axis, [(i, i + 1) for i in range(first, lax.axis_size...  5.99 us
    ppermute x2, starting transfers between devices, swap(): return lax.ppermute(block, axis, route)  4.29 us
  transfers between devices with their start and end apart: 4, of which 1 were waited for; matrix products, arithmetic and copies ran while one was open for 0% of the time, Pallas kernels for 20%

profile of v2, /device:TPU:0, one launch (start us, length us, event | category | flops | bytes accessed | tf_op | source)
XLA Modules:
  0.0 91.2 jit_solution(16529885246156073257)
XLA Ops:
  0.0 8.4 %shard_map.65 = (bf16[768,768]{1,0:T(8,128)(2,1)S(1)}, bf16[768,768]{1,0:T(8,128)(2,1)S(1)}, bf16[768,768]{1,0:T(8,128)(2,1)S(1)}, bf16[768,768]{1,0:T(8,128)(2,...) custom-call(f32[1,2,1,2,384,384]{5,4,3,2,1,0:T(8,128)} %diag.1, ...), custom_call_target="tpu_custom_call" | custom-call | flops 30000001024 | bytes 1 | tf_op jit(solution)/shard_map/pallas_call | solution.py:370
  8.4 0.7 collective-permute-start
  9.1 3.7 %shard_map.66 = (bf16[384,768]{1,0:T(8,128)(2,1)S(1)}, bf16[384,768]{1,0:T(8,128)(2,1)S(1)}, f32[384,768]{1,0:T(8,128)S(1)}) custom-call(f32[2,384,384]{2,1,0:T(8,128)S(1)} %get-tuple-element.28.even, bf16[768,768]{1,0:T(8,128)(2,1)S(1)} %get-tuple-element.29.refs_0_, bf16[768,768]{1,0:T(8,128)(2,1)S(1)} %get-tuple-element.30.refs_1_, ...), custom_call_target="tpu_custom_call" | custom-call | flops 30000001024 | bytes 1 | tf_op jit(solution)/shard_map/pallas_call | solution.py:370
  12.9 3.5 %collective-permute-start.1 = (f32[384,768]{1,0:T(8,128)S(1)}, f32[384,768]{1,0:T(8,128)S(1)}, u32[]{:S(2)}, u32[]{:S(2)}) collective-permute-start(f32[384,768]{1,0:T(8,128)S(1)} %get-tuple-element.46.mine), channel_id=1, source_target_pairs={{0,16},{16,0},{32,48},{48,32},{64,80},{80,64},{96,112},{112,96},{1... | collective-permute-start | bytes 3538952 | tf_op jit(solution)/shard_map/ppermute | solution.py:386
  16.4 2.9 %shard_map.67 = (f32[384,768]{1,0:T(8,128)S(1)}, f32[384,768]{1,0:T(8,128)S(1)}) custom-call(bf16[384,768]{1,0:T(8,128)(2,1)S(1)} %get-tuple-element.38.refs_0_, bf16[384,768]{1,0:T(8,128)(2,1)S(1)} %get-tuple-element.39.refs_1_, bf16[768,768]{1,0:T(8,128)(2,1)S(1)} %get-tuple-element.40.refs_2_, bf16[768,768]{1,0:T(8,128)(2,1)S(1)} %get-tuple-element.41.refs_3_, ...), custom_call_target="tpu_custom_call" | custom-call | flops 30000001024 | bytes 1 | tf_op jit(solution)/shard_map/pallas_call | solution.py:370
  19.3 0.0 collective-permute-done.1.far
  19.3 5.3 %shard_map.68 = (f32[384,768]{1,0:T(8,128)S(1)}, f32[384,768]{1,0:T(8,128)S(1)}) custom-call(f32[384,768]{1,0:T(8,128)S(1)} %get-tuple-element.46.mine, f32[384,768]{1,0:T(8,128)S(1)} %collective-permute-done.1.far, f32[384,768]{1,0:T(8,128)S(1)} %get-tuple-element.44.one, f32[384,768]{1,0:T(8,128)S(1)} %get-tuple-element.45.two), custom_call_target="tpu_custom_call" | custom-call | flops 30000001024 | bytes 1 | tf_op jit(solution)/shard_map/pallas_call | solution.py:370
  24.6 0.7 collective-permute-start.2
  25.4 0.0 collective-permute-done.far
  25.4 0.0 copy-start
  25.4 0.0 copy-start.1
  25.4 0.0 copy-start.2
  25.4 0.0 copy-start.3
  25.4 5.3 %shard_map.69 = (f32[384,768]{1,0:T(8,128)S(1)}, f32[384,768]{1,0:T(8,128)S(1)}) custom-call(f32[384,768]{1,0:T(8,128)S(1)} %get-tuple-element.37.mine, f32[384,768]{1,0:T(8,128)S(1)} %collective-permute-done.far, f32[384,768]{1,0:T(8,128)S(1)} %get-tuple-element.44.one, f32[384,768]{1,0:T(8,128)S(1)} %get-tuple-element.45.two, ...), custom_call_target="tpu_custom_call" | custom-call | flops 30000001024 | bytes 1 | tf_op jit(solution)/shard_map/pallas_call | solution.py:370
  30.8 5.3 %collective-permute-start.3 = (f32[384,768]{1,0:T(8,128)S(1)}, f32[384,768]{1,0:T(8,128)S(1)}, u32[]{:S(2)}, u32[]{:S(2)}) collective-permute-start(f32[384,768]{1,0:T(8,128)S(1)} %get-tuple-element.50), channel_id=1, source_target_pairs={{0,16},{32,48},{64,80},{96,112},{1,17},{33,49},{65,81},{97,113},{2... | collective-permute-start | bytes 3538952 | tf_op jit(solution)/shard_map/ppermute | solution.py:390
  36.0 0.0 copy-done
  36.0 0.0 copy-done.1
  36.1 0.0 copy-done.2
  36.1 0.0 copy-done.3
  36.1 0.6 shard_map.64.weights
  36.7 1.7 %collective-permute-done.3.chip_term = f32[384,768]{1,0:T(8,128)S(1)} collective-permute-done((f32[384,768]{1,0:T(8,128)S(1)}, f32[384,768]{1,0:T(8,128)S(1)}, u32[]{:S(2)}, u32[]{:S(2)}) %collective-permute-start.3) | collective-permute-done | bytes 1179680 | tf_op jit(solution)/shard_map/ppermute | solution.py:390
  38.4 0.0 collective-permute-done.2.border_term
  38.4 3.6 %shard_map.71 = f32[2,384,384]{2,1,0:T(8,128)S(1)} custom-call(f32[384,768]{1,0:T(8,128)S(1)} %get-tuple-element.49.partial, f32[384,768]{1,0:T(8,128)S(1)} %collective-permute-done.2.border_term, f32[2,384,384]{2,1,0:T(8,128)S(1)} %shard_map.70.odd_greens), custom_call_target="tpu_custom_call", output_to_operand_aliasing={{}: (2, {})} | custom-call | flops 30000001024 | bytes 1 | tf_op jit(solution)/shard_map/pallas_call | solution.py:370
  42.0 26.0 %all_to_all.10 = f32[16,48,384]{2,1,0:T(8,128)S(1)} all-to-all(f32[16,48,384]{2,1,0:T(8,128)S(1)} %bitcast.6), channel_id=1, replica_groups=mesh['layer'=8,'energy'=4,'momentum'=4] {'energy','momentum'}, dimensions={0} | all-to-all | bytes 2359296 | tf_op jit(solution)/shard_map/all_to_all | solution.py:443
  68.0 1.0 %shard_map.72 = f32[4,4,48,384]{3,2,1,0:T(8,128)S(1)} custom-call(f32[24,128]{1,0:T(8,128)S(1)} %shard_map.64.weights, f32[4,4,48,384]{3,2,1,0:T(8,128)S(1)} %bitcast.4), custom_call_target="tpu_custom_call" | custom-call | tf_op jit(solution)/shard_map/pallas_call | solution.py:447
  69.0 21.2 %all_to_all.11 = f32[16,48,384]{2,1,0:T(8,128)S(1)} all-to-all(f32[16,48,384]{2,1,0:T(8,128)S(1)} %bitcast.5), channel_id=1, replica_groups=mesh['layer'=8,'energy'=4,'momentum'=4] {'energy','momentum'}, dimensions={0} | all-to-all | bytes 2359296 | tf_op jit(solution)/shard_map/all_to_all | solution.py:454
  90.2 1.0 %copy.10 = f32[1,1,1,2,384,384]{5,4,3,2,1,0:T(8,128)} copy(f32[1,1,1,2,384,384]{5,4,3,2,1,0:T(8,128)S(1)} %bitcast.7) | data formatting | bytes 2359296
  (1 shorter events, 0.0 us)
Async XLA Ops:
  8.4 17.0 %collective-permute-start = (f32[384,768]{1,0:T(8,128)S(1)}, f32[384,768]{1,0:T(8,128)S(1)}, u32[]{:S(2)}, u32[]{:S(2)}) collective-permute-start(f32[384,768]{1,0:T(8,128)S(1)} %get-tuple-element.37.mine), channel_id=1, source_target_pairs={{16,32},{32,16},{48,64},{64,48},{80,96},{96,80},{17,33},{33,17},{4... | collective-permute-start | bytes 3538952 | tf_op jit(solution)/shard_map/ppermute | solution.py:386
  12.9 6.5 %collective-permute-start.1 = (f32[384,768]{1,0:T(8,128)S(1)}, f32[384,768]{1,0:T(8,128)S(1)}, u32[]{:S(2)}, u32[]{:S(2)}) collective-permute-start(f32[384,768]{1,0:T(8,128)S(1)} %get-tuple-element.46.mine), channel_id=1, source_target_pairs={{0,16},{16,0},{32,48},{48,32},{64,80},{80,64},{96,112},{112,96},{1... | collective-permute-start | bytes 3538952 | tf_op jit(solution)/shard_map/ppermute | solution.py:386
  24.6 13.8 %collective-permute-start.2 = (f32[384,768]{1,0:T(8,128)S(1)}, f32[384,768]{1,0:T(8,128)S(1)}, u32[]{:S(2)}, u32[]{:S(2)}) collective-permute-start(f32[384,768]{1,0:T(8,128)S(1)} %get-tuple-element.48.chip_term), channel_id=1, source_target_pairs={{16,32},{48,64},{80,96},{17,33},{49,65},{81,97},{18,34},{50,66},{8... | collective-permute-start | bytes 3538952 | tf_op jit(solution)/shard_map/ppermute | solution.py:390
  25.4 10.6 %copy-start = (f32[4,4]{1,0:T(4,128)S(1)}, f32[4,4]{1,0:T(4,128)}, u32[]{:S(2)}) copy-start(f32[4,4]{1,0:T(4,128)} %phonon.1) | copy-start | bytes 196
  25.4 10.6 %copy-start.1 = (f32[3]{0:T(128)S(1)}, f32[3]{0:T(128)}, u32[]{:S(2)}) copy-start(f32[3]{0:T(128)} %strength.1) | copy-start | bytes 40
  25.4 10.6 %copy-start.2 = (s32[4]{0:T(128)S(1)}, s32[4]{0:T(128)}, u32[]{:S(2)}) copy-start(s32[4]{0:T(128)} %transfer.1) | copy-start | bytes 52
  25.4 10.6 %copy-start.3 = (s32[3]{0:T(128)S(1)}, s32[3]{0:T(128)}, u32[]{:S(2)}) copy-start(s32[3]{0:T(128)} %offset.1) | copy-start | bytes 40
  30.8 7.6 %collective-permute-start.3 = (f32[384,768]{1,0:T(8,128)S(1)}, f32[384,768]{1,0:T(8,128)S(1)}, u32[]{:S(2)}, u32[]{:S(2)}) collective-permute-start(f32[384,768]{1,0:T(8,128)S(1)} %get-tuple-element.50), channel_id=1, source_target_pairs={{0,16},{32,48},{64,80},{96,112},{1,17},{33,49},{65,81},{97,113},{2... | collective-permute-start | bytes 3538952 | tf_op jit(solution)/shard_map/ppermute | solution.py:390

commit v3 on v2

--- a/solution.py
+++ b/solution.py
@@ -182,9 +182,10 @@
     for copy in urgent:
         copy.start()
 
+    later[0].start()
     for copy in urgent:
         copy.wait()
-    for copy in later:
+    for copy in later[1:]:
         copy.start()
 
     def chunk(at):
@@ -356,7 +357,7 @@
                     mixed[e, k, rows, columns] = total
             return carry
 
-        lax.fori_loop(0, depth // 8, rows_of, 0, unroll=2)
+        lax.fori_loop(0, depth // 8, rows_of, 0, unroll=True)
 
 
 def call(kernel, outs, operands, scratch=(), aliases=()):

time: 91.5 us -> 90.8 us (level)
  no operation moved by 1% of the time
where the time goes in v3:
time: 90.8 us; the launch traced here: 90.5 us
  blocking collectives  47.3 us (52%)
  Pallas kernels  30.1 us (33%)
  starting transfers between devices  10.3 us (11%)
  waiting for transfers between devices  1.74 us (2%)
  local copies, waits for them, and re-layouts  1.04 us (1%)
    pallas_call x8, Pallas kernels, call(): pl.pallas_call(kernel, out_shape=outs, in_specs=[spec(o) for o in operand...  29.2 us
    all_to_all x1, blocking collectives, body(): lax.all_to_all(greens.reshape(group, depth, n), axes, split_axis=0, conca...  26 us
    all_to_all x1, blocking collectives, body(): lax.all_to_all(mixed.reshape(group, depth, n), axes, split_axis=0, concat...  21.2 us
    ppermute x2, starting transfers between devices, ahead(): lax.ppermute(block, axis, [(i, i + 1) for i in range(first, lax.axis_size...  5.99 us
    ppermute x2, starting transfers between devices, swap(): return lax.ppermute(block, axis, route)  4.28 us
  transfers between devices with their start and end apart: 4, of which 1 were waited for; matrix products, arithmetic and copies ran while one was open for 0% of the time, Pallas kernels for 20%

profile of v3, /device:TPU:0, one launch (start us, length us, event | category | flops | bytes accessed | tf_op | source)
XLA Modules:
  0.0 90.5 jit_solution(15247907360086725818)
XLA Ops:
  0.0 7.8 %shard_map.65 = (bf16[768,768]{1,0:T(8,128)(2,1)S(1)}, bf16[768,768]{1,0:T(8,128)(2,1)S(1)}, bf16[768,768]{1,0:T(8,128)(2,1)S(1)}, bf16[768,768]{1,0:T(8,128)(2,...) custom-call(f32[1,2,1,2,384,384]{5,4,3,2,1,0:T(8,128)} %diag.1, ...), custom_call_target="tpu_custom_call" | custom-call | flops 30000001024 | bytes 1 | tf_op jit(solution)/shard_map/pallas_call | solution.py:371
  7.8 0.7 collective-permute-start
  8.5 3.7 %shard_map.66 = (bf16[384,768]{1,0:T(8,128)(2,1)S(1)}, bf16[384,768]{1,0:T(8,128)(2,1)S(1)}, f32[384,768]{1,0:T(8,128)S(1)}) custom-call(f32[2,384,384]{2,1,0:T(8,128)S(1)} %get-tuple-element.28.even, bf16[768,768]{1,0:T(8,128)(2,1)S(1)} %get-tuple-element.29.refs_0_, bf16[768,768]{1,0:T(8,128)(2,1)S(1)} %get-tuple-element.30.refs_1_, ...), custom_call_target="tpu_custom_call" | custom-call | flops 30000001024 | bytes 1 | tf_op jit(solution)/shard_map/pallas_call | solution.py:371
  12.2 3.5 %collective-permute-start.1 = (f32[384,768]{1,0:T(8,128)S(1)}, f32[384,768]{1,0:T(8,128)S(1)}, u32[]{:S(2)}, u32[]{:S(2)}) collective-permute-start(f32[384,768]{1,0:T(8,128)S(1)} %get-tuple-element.46.mine), channel_id=1, source_target_pairs={{0,16},{16,0},{32,48},{48,32},{64,80},{80,64},{96,112},{112,96},{1... | collective-permute-start | bytes 3538952 | tf_op jit(solution)/shard_map/ppermute | solution.py:387
  15.8 2.9 %shard_map.67 = (f32[384,768]{1,0:T(8,128)S(1)}, f32[384,768]{1,0:T(8,128)S(1)}) custom-call(bf16[384,768]{1,0:T(8,128)(2,1)S(1)} %get-tuple-element.38.refs_0_, bf16[384,768]{1,0:T(8,128)(2,1)S(1)} %get-tuple-element.39.refs_1_, bf16[768,768]{1,0:T(8,128)(2,1)S(1)} %get-tuple-element.40.refs_2_, bf16[768,768]{1,0:T(8,128)(2,1)S(1)} %get-tuple-element.41.refs_3_, ...), custom_call_target="tpu_custom_call" | custom-call | flops 30000001024 | bytes 1 | tf_op jit(solution)/shard_map/pallas_call | solution.py:371
  18.7 0.0 collective-permute-done.1.far
  18.7 5.3 %shard_map.68 = (f32[384,768]{1,0:T(8,128)S(1)}, f32[384,768]{1,0:T(8,128)S(1)}) custom-call(f32[384,768]{1,0:T(8,128)S(1)} %get-tuple-element.46.mine, f32[384,768]{1,0:T(8,128)S(1)} %collective-permute-done.1.far, f32[384,768]{1,0:T(8,128)S(1)} %get-tuple-element.44.one, f32[384,768]{1,0:T(8,128)S(1)} %get-tuple-element.45.two), custom_call_target="tpu_custom_call" | custom-call | flops 30000001024 | bytes 1 | tf_op jit(solution)/shard_map/pallas_call | solution.py:371
  24.0 0.7 collective-permute-start.2
  24.8 0.0 collective-permute-done.far
  24.8 0.0 copy-start
  24.8 0.0 copy-start.1
  24.8 0.0 copy-start.2
  24.8 0.0 copy-start.3
  24.8 5.3 %shard_map.69 = (f32[384,768]{1,0:T(8,128)S(1)}, f32[384,768]{1,0:T(8,128)S(1)}) custom-call(f32[384,768]{1,0:T(8,128)S(1)} %get-tuple-element.37.mine, f32[384,768]{1,0:T(8,128)S(1)} %collective-permute-done.far, f32[384,768]{1,0:T(8,128)S(1)} %get-tuple-element.44.one, f32[384,768]{1,0:T(8,128)S(1)} %get-tuple-element.45.two, ...), custom_call_target="tpu_custom_call" | custom-call | flops 30000001024 | bytes 1 | tf_op jit(solution)/shard_map/pallas_call | solution.py:371
  30.2 5.3 %collective-permute-start.3 = (f32[384,768]{1,0:T(8,128)S(1)}, f32[384,768]{1,0:T(8,128)S(1)}, u32[]{:S(2)}, u32[]{:S(2)}) collective-permute-start(f32[384,768]{1,0:T(8,128)S(1)} %get-tuple-element.50), channel_id=1, source_target_pairs={{0,16},{32,48},{64,80},{96,112},{1,17},{33,49},{65,81},{97,113},{2... | collective-permute-start | bytes 3538952 | tf_op jit(solution)/shard_map/ppermute | solution.py:391
  35.4 0.0 copy-done
  35.4 0.0 copy-done.1
  35.4 0.0 copy-done.2
  35.4 0.0 copy-done.3
  35.5 0.6 shard_map.64.weights
  36.1 1.7 %collective-permute-done.3.chip_term = f32[384,768]{1,0:T(8,128)S(1)} collective-permute-done((f32[384,768]{1,0:T(8,128)S(1)}, f32[384,768]{1,0:T(8,128)S(1)}, u32[]{:S(2)}, u32[]{:S(2)}) %collective-permute-start.3) | collective-permute-done | bytes 1179680 | tf_op jit(solution)/shard_map/ppermute | solution.py:391
  37.8 0.0 collective-permute-done.2.border_term
  37.8 3.6 %shard_map.71 = f32[2,384,384]{2,1,0:T(8,128)S(1)} custom-call(f32[384,768]{1,0:T(8,128)S(1)} %get-tuple-element.49.partial, f32[384,768]{1,0:T(8,128)S(1)} %collective-permute-done.2.border_term, f32[2,384,384]{2,1,0:T(8,128)S(1)} %shard_map.70.odd_greens), custom_call_target="tpu_custom_call", output_to_operand_aliasing={{}: (2, {})} | custom-call | flops 30000001024 | bytes 1 | tf_op jit(solution)/shard_map/pallas_call | solution.py:371
  41.4 26.0 %all_to_all.10 = f32[16,48,384]{2,1,0:T(8,128)S(1)} all-to-all(f32[16,48,384]{2,1,0:T(8,128)S(1)} %bitcast.6), channel_id=1, replica_groups=mesh['layer'=8,'energy'=4,'momentum'=4] {'energy','momentum'}, dimensions={0} | all-to-all | bytes 2359296 | tf_op jit(solution)/shard_map/all_to_all | solution.py:444
  67.4 0.9 shard_map.72
  68.3 21.2 %all_to_all.11 = f32[16,48,384]{2,1,0:T(8,128)S(1)} all-to-all(f32[16,48,384]{2,1,0:T(8,128)S(1)} %bitcast.5), channel_id=1, replica_groups=mesh['layer'=8,'energy'=4,'momentum'=4] {'energy','momentum'}, dimensions={0} | all-to-all | bytes 2359296 | tf_op jit(solution)/shard_map/all_to_all | solution.py:455
  89.5 1.0 %copy.10 = f32[1,1,1,2,384,384]{5,4,3,2,1,0:T(8,128)} copy(f32[1,1,1,2,384,384]{5,4,3,2,1,0:T(8,128)S(1)} %bitcast.7) | data formatting | bytes 2359296
  (1 shorter events, 0.0 us)
Async XLA Ops:
  7.8 17.0 %collective-permute-start = (f32[384,768]{1,0:T(8,128)S(1)}, f32[384,768]{1,0:T(8,128)S(1)}, u32[]{:S(2)}, u32[]{:S(2)}) collective-permute-start(f32[384,768]{1,0:T(8,128)S(1)} %get-tuple-element.37.mine), channel_id=1, source_target_pairs={{16,32},{32,16},{48,64},{64,48},{80,96},{96,80},{17,33},{33,17},{4... | collective-permute-start | bytes 3538952 | tf_op jit(solution)/shard_map/ppermute | solution.py:387
  12.2 6.5 %collective-permute-start.1 = (f32[384,768]{1,0:T(8,128)S(1)}, f32[384,768]{1,0:T(8,128)S(1)}, u32[]{:S(2)}, u32[]{:S(2)}) collective-permute-start(f32[384,768]{1,0:T(8,128)S(1)} %get-tuple-element.46.mine), channel_id=1, source_target_pairs={{0,16},{16,0},{32,48},{48,32},{64,80},{80,64},{96,112},{112,96},{1... | collective-permute-start | bytes 3538952 | tf_op jit(solution)/shard_map/ppermute | solution.py:387
  24.0 13.8 %collective-permute-start.2 = (f32[384,768]{1,0:T(8,128)S(1)}, f32[384,768]{1,0:T(8,128)S(1)}, u32[]{:S(2)}, u32[]{:S(2)}) collective-permute-start(f32[384,768]{1,0:T(8,128)S(1)} %get-tuple-element.48.chip_term), channel_id=1, source_target_pairs={{16,32},{48,64},{80,96},{17,33},{49,65},{81,97},{18,34},{50,66},{8... | collective-permute-start | bytes 3538952 | tf_op jit(solution)/shard_map/ppermute | solution.py:391
  24.8 10.6 %copy-start = (f32[4,4]{1,0:T(4,128)S(1)}, f32[4,4]{1,0:T(4,128)}, u32[]{:S(2)}) copy-start(f32[4,4]{1,0:T(4,128)} %phonon.1) | copy-start | bytes 196
  24.8 10.6 %copy-start.1 = (f32[3]{0:T(128)S(1)}, f32[3]{0:T(128)}, u32[]{:S(2)}) copy-start(f32[3]{0:T(128)} %strength.1) | copy-start | bytes 40
  24.8 10.6 %copy-start.2 = (s32[4]{0:T(128)S(1)}, s32[4]{0:T(128)}, u32[]{:S(2)}) copy-start(s32[4]{0:T(128)} %transfer.1) | copy-start | bytes 52
  24.8 10.6 %copy-start.3 = (s32[3]{0:T(128)S(1)}, s32[3]{0:T(128)}, u32[]{:S(2)}) copy-start(s32[3]{0:T(128)} %offset.1) | copy-start | bytes 40
  30.2 7.6 %collective-permute-start.3 = (f32[384,768]{1,0:T(8,128)S(1)}, f32[384,768]{1,0:T(8,128)S(1)}, u32[]{:S(2)}, u32[]{:S(2)}) collective-permute-start(f32[384,768]{1,0:T(8,128)S(1)} %get-tuple-element.50), channel_id=1, source_target_pairs={{0,16},{32,48},{64,80},{96,112},{1,17},{33,49},{65,81},{97,113},{2... | collective-permute-start | bytes 3538952 | tf_op jit(solution)/shard_map/ppermute | solution.py:391

commit v4 on v3

--- a/solution.py
+++ b/solution.py
@@ -121,7 +121,7 @@
         q_imag = rest[:, imag_of(at)] - imag
         epilogue(at, col_real * q_real - col_imag * q_imag, col_real * q_imag + col_imag * q_real)
 
-    product(left, second, finish, more)
+    product(left[: len(second)], second, finish, more)
 
 
 def pairs_of(refs):
@@ -201,8 +201,8 @@
     near_fill = factors(which, near, other, right)
     refined_inverse(
         chunk,
-        left[:1],
-        first[:1],
+        left,
+        first,
         second[:1],
         rest,
         lambda at, real, imag: put_right(inverse, at, real, imag),

time: 90.8 us -> 91.9 us (1.012)
  Pallas kernels: 30.1 us -> 31.2 us
    pallas_call x8, Pallas kernels: 29.2 us -> 30.3 us  [call(): pl.pallas_call(kernel, out_shape=outs, in_specs=[spec(o) for o in operand...]
  transfers between devices with their start and end apart: 4 -> 4, of which waited for: 1 -> 1; matrix products, arithmetic and copies ran while one was open for 0% -> 0% of each run, Pallas kernels for 20% -> 19%
where the time goes in v4:
time: 91.9 us; the launch traced here: 91.6 us
  blocking collectives  47.3 us (51%)
  Pallas kernels  31.2 us (34%)
  starting transfers between devices  10.3 us (11%)
  waiting for transfers between devices  1.74 us (2%)
  local copies, waits for them, and re-layouts  1.04 us (1%)
    pallas_call x8, Pallas kernels, call(): pl.pallas_call(kernel, out_shape=outs, in_specs=[spec(o) for o in operand...  30.3 us
    all_to_all x1, blocking collectives, body(): lax.all_to_all(greens.reshape(group, depth, n), axes, split_axis=0, conca...  26 us
    all_to_all x1, blocking collectives, body(): lax.all_to_all(mixed.reshape(group, depth, n), axes, split_axis=0, concat...  21.2 us
    ppermute x2, starting transfers between devices, ahead(): lax.ppermute(block, axis, [(i, i + 1) for i in range(first, lax.axis_size...  5.99 us
    ppermute x2, starting transfers between devices, swap(): return lax.ppermute(block, axis, route)  4.28 us
  transfers between devices with their start and end apart: 4, of which 1 were waited for; matrix products, arithmetic and copies ran while one was open for 0% of the time, Pallas kernels for 19%

profile of v4, /device:TPU:0, one launch (start us, length us, event | category | flops | bytes accessed | tf_op | source)
XLA Modules:
  0.0 91.6 jit_solution(4364522912741062730)
XLA Ops:
  0.0 8.9 %shard_map.65 = (bf16[768,768]{1,0:T(8,128)(2,1)S(1)}, bf16[768,768]{1,0:T(8,128)(2,1)S(1)}, bf16[768,768]{1,0:T(8,128)(2,1)S(1)}, bf16[768,768]{1,0:T(8,128)(2,...) custom-call(f32[1,2,1,2,384,384]{5,4,3,2,1,0:T(8,128)} %diag.1, ...), custom_call_target="tpu_custom_call" | custom-call | flops 30000001024 | bytes 1 | tf_op jit(solution)/shard_map/pallas_call | solution.py:371
  8.9 0.7 collective-permute-start
  9.6 3.7 %shard_map.66 = (bf16[384,768]{1,0:T(8,128)(2,1)S(1)}, bf16[384,768]{1,0:T(8,128)(2,1)S(1)}, f32[384,768]{1,0:T(8,128)S(1)}) custom-call(f32[2,384,384]{2,1,0:T(8,128)S(1)} %get-tuple-element.28.even, bf16[768,768]{1,0:T(8,128)(2,1)S(1)} %get-tuple-element.29.refs_0_, bf16[768,768]{1,0:T(8,128)(2,1)S(1)} %get-tuple-element.30.refs_1_, ...), custom_call_target="tpu_custom_call" | custom-call | flops 30000001024 | bytes 1 | tf_op jit(solution)/shard_map/pallas_call | solution.py:371
  13.3 3.5 %collective-permute-start.1 = (f32[384,768]{1,0:T(8,128)S(1)}, f32[384,768]{1,0:T(8,128)S(1)}, u32[]{:S(2)}, u32[]{:S(2)}) collective-permute-start(f32[384,768]{1,0:T(8,128)S(1)} %get-tuple-element.46.mine), channel_id=1, source_target_pairs={{0,16},{16,0},{32,48},{48,32},{64,80},{80,64},{96,112},{112,96},{1... | collective-permute-start | bytes 3538952 | tf_op jit(solution)/shard_map/ppermute | solution.py:387
  16.9 2.9 %shard_map.67 = (f32[384,768]{1,0:T(8,128)S(1)}, f32[384,768]{1,0:T(8,128)S(1)}) custom-call(bf16[384,768]{1,0:T(8,128)(2,1)S(1)} %get-tuple-element.38.refs_0_, bf16[384,768]{1,0:T(8,128)(2,1)S(1)} %get-tuple-element.39.refs_1_, bf16[768,768]{1,0:T(8,128)(2,1)S(1)} %get-tuple-element.40.refs_2_, bf16[768,768]{1,0:T(8,128)(2,1)S(1)} %get-tuple-element.41.refs_3_, ...), custom_call_target="tpu_custom_call" | custom-call | flops 30000001024 | bytes 1 | tf_op jit(solution)/shard_map/pallas_call | solution.py:371
  19.8 0.0 collective-permute-done.1.far
  19.8 5.3 %shard_map.68 = (f32[384,768]{1,0:T(8,128)S(1)}, f32[384,768]{1,0:T(8,128)S(1)}) custom-call(f32[384,768]{1,0:T(8,128)S(1)} %get-tuple-element.46.mine, f32[384,768]{1,0:T(8,128)S(1)} %collective-permute-done.1.far, f32[384,768]{1,0:T(8,128)S(1)} %get-tuple-element.44.one, f32[384,768]{1,0:T(8,128)S(1)} %get-tuple-element.45.two), custom_call_target="tpu_custom_call" | custom-call | flops 30000001024 | bytes 1 | tf_op jit(solution)/shard_map/pallas_call | solution.py:371
  25.1 0.7 collective-permute-start.2
  25.9 0.0 collective-permute-done.far
  25.9 0.0 copy-start
  25.9 0.0 copy-start.1
  25.9 0.0 copy-start.2
  25.9 0.0 copy-start.3
  25.9 5.3 %shard_map.69 = (f32[384,768]{1,0:T(8,128)S(1)}, f32[384,768]{1,0:T(8,128)S(1)}) custom-call(f32[384,768]{1,0:T(8,128)S(1)} %get-tuple-element.37.mine, f32[384,768]{1,0:T(8,128)S(1)} %collective-permute-done.far, f32[384,768]{1,0:T(8,128)S(1)} %get-tuple-element.44.one, f32[384,768]{1,0:T(8,128)S(1)} %get-tuple-element.45.two, ...), custom_call_target="tpu_custom_call" | custom-call | flops 30000001024 | bytes 1 | tf_op jit(solution)/shard_map/pallas_call | solution.py:371
  31.3 5.3 %collective-permute-start.3 = (f32[384,768]{1,0:T(8,128)S(1)}, f32[384,768]{1,0:T(8,128)S(1)}, u32[]{:S(2)}, u32[]{:S(2)}) collective-permute-start(f32[384,768]{1,0:T(8,128)S(1)} %get-tuple-element.50), channel_id=1, source_target_pairs={{0,16},{32,48},{64,80},{96,112},{1,17},{33,49},{65,81},{97,113},{2... | collective-permute-start | bytes 3538952 | tf_op jit(solution)/shard_map/ppermute | solution.py:391
  36.5 0.0 copy-done
  36.5 0.0 copy-done.1
  36.5 0.0 copy-done.2
  36.6 0.0 copy-done.3
  36.6 0.6 shard_map.64.weights
  37.2 1.7 %collective-permute-done.3.chip_term = f32[384,768]{1,0:T(8,128)S(1)} collective-permute-done((f32[384,768]{1,0:T(8,128)S(1)}, f32[384,768]{1,0:T(8,128)S(1)}, u32[]{:S(2)}, u32[]{:S(2)}) %collective-permute-start.3) | collective-permute-done | bytes 1179680 | tf_op jit(solution)/shard_map/ppermute | solution.py:391
  38.9 0.0 collective-permute-done.2.border_term
  38.9 3.6 %shard_map.71 = f32[2,384,384]{2,1,0:T(8,128)S(1)} custom-call(f32[384,768]{1,0:T(8,128)S(1)} %get-tuple-element.49.partial, f32[384,768]{1,0:T(8,128)S(1)} %collective-permute-done.2.border_term, f32[2,384,384]{2,1,0:T(8,128)S(1)} %shard_map.70.odd_greens), custom_call_target="tpu_custom_call", output_to_operand_aliasing={{}: (2, {})} | custom-call | flops 30000001024 | bytes 1 | tf_op jit(solution)/shard_map/pallas_call | solution.py:371
  42.5 26.0 %all_to_all.10 = f32[16,48,384]{2,1,0:T(8,128)S(1)} all-to-all(f32[16,48,384]{2,1,0:T(8,128)S(1)} %bitcast.6), channel_id=1, replica_groups=mesh['layer'=8,'energy'=4,'momentum'=4] {'energy','momentum'}, dimensions={0} | all-to-all | bytes 2359296 | tf_op jit(solution)/shard_map/all_to_all | solution.py:444
  68.5 0.9 shard_map.72
  69.4 21.2 %all_to_all.11 = f32[16,48,384]{2,1,0:T(8,128)S(1)} all-to-all(f32[16,48,384]{2,1,0:T(8,128)S(1)} %bitcast.5), channel_id=1, replica_groups=mesh['layer'=8,'energy'=4,'momentum'=4] {'energy','momentum'}, dimensions={0} | all-to-all | bytes 2359296 | tf_op jit(solution)/shard_map/all_to_all | solution.py:455
  90.6 1.0 %copy.10 = f32[1,1,1,2,384,384]{5,4,3,2,1,0:T(8,128)} copy(f32[1,1,1,2,384,384]{5,4,3,2,1,0:T(8,128)S(1)} %bitcast.7) | data formatting | bytes 2359296
  (1 shorter events, 0.0 us)
Async XLA Ops:
  8.9 17.0 %collective-permute-start = (f32[384,768]{1,0:T(8,128)S(1)}, f32[384,768]{1,0:T(8,128)S(1)}, u32[]{:S(2)}, u32[]{:S(2)}) collective-permute-start(f32[384,768]{1,0:T(8,128)S(1)} %get-tuple-element.37.mine), channel_id=1, source_target_pairs={{16,32},{32,16},{48,64},{64,48},{80,96},{96,80},{17,33},{33,17},{4... | collective-permute-start | bytes 3538952 | tf_op jit(solution)/shard_map/ppermute | solution.py:387
  13.3 6.5 %collective-permute-start.1 = (f32[384,768]{1,0:T(8,128)S(1)}, f32[384,768]{1,0:T(8,128)S(1)}, u32[]{:S(2)}, u32[]{:S(2)}) collective-permute-start(f32[384,768]{1,0:T(8,128)S(1)} %get-tuple-element.46.mine), channel_id=1, source_target_pairs={{0,16},{16,0},{32,48},{48,32},{64,80},{80,64},{96,112},{112,96},{1... | collective-permute-start | bytes 3538952 | tf_op jit(solution)/shard_map/ppermute | solution.py:387
  25.1 13.8 %collective-permute-start.2 = (f32[384,768]{1,0:T(8,128)S(1)}, f32[384,768]{1,0:T(8,128)S(1)}, u32[]{:S(2)}, u32[]{:S(2)}) collective-permute-start(f32[384,768]{1,0:T(8,128)S(1)} %get-tuple-element.48.chip_term), channel_id=1, source_target_pairs={{16,32},{48,64},{80,96},{17,33},{49,65},{81,97},{18,34},{50,66},{8... | collective-permute-start | bytes 3538952 | tf_op jit(solution)/shard_map/ppermute | solution.py:391
  25.9 10.6 %copy-start = (f32[4,4]{1,0:T(4,128)S(1)}, f32[4,4]{1,0:T(4,128)}, u32[]{:S(2)}) copy-start(f32[4,4]{1,0:T(4,128)} %phonon.1) | copy-start | bytes 196
  25.9 10.6 %copy-start.1 = (f32[3]{0:T(128)S(1)}, f32[3]{0:T(128)}, u32[]{:S(2)}) copy-start(f32[3]{0:T(128)} %strength.1) | copy-start | bytes 40
  25.9 10.6 %copy-start.2 = (s32[4]{0:T(128)S(1)}, s32[4]{0:T(128)}, u32[]{:S(2)}) copy-start(s32[4]{0:T(128)} %transfer.1) | copy-start | bytes 52
  25.9 10.6 %copy-start.3 = (s32[3]{0:T(128)S(1)}, s32[3]{0:T(128)}, u32[]{:S(2)}) copy-start(s32[3]{0:T(128)} %offset.1) | copy-start | bytes 40
  31.3 7.6 %collective-permute-start.3 = (f32[384,768]{1,0:T(8,128)S(1)}, f32[384,768]{1,0:T(8,128)S(1)}, u32[]{:S(2)}, u32[]{:S(2)}) collective-permute-start(f32[384,768]{1,0:T(8,128)S(1)} %get-tuple-element.50), channel_id=1, source_target_pairs={{0,16},{32,48},{64,80},{96,112},{1,17},{33,49},{65,81},{97,113},{2... | collective-permute-start | bytes 3538952 | tf_op jit(solution)/shard_map/ppermute | solution.py:391

commit v5 on v3

--- a/solution.py
+++ b/solution.py
@@ -328,7 +328,7 @@
 
 
 def mix_kernel(weights, blocks, mixed):
-    energies, momenta, depth, width = blocks.shape
+    momenta, energies, depth, width = blocks.shape
     rows = [weights[row : row + 1, :] for row in range(energies * energies + 2 * momenta)]
     fold = [rows[e * energies : (e + 1) * energies] for e in range(energies)]
     stay, move = rows[-2 * momenta : -momenta], rows[-momenta:]
@@ -339,7 +339,7 @@
             rows = pl.ds(pl.multiple_of(i * 8, 8), 8)
             folded = []
             for k in range(momenta):
-                g = [blocks[f, k, rows, columns] for f in range(energies)]
+                g = [blocks[k, f, rows, columns] for f in range(energies)]
                 folded.append(
                     [sum(fold[e][f] * g[f] for f in range(energies)) for e in range(energies)]
                 )
@@ -354,7 +354,7 @@
                         total = total + moved[e - 1]
                     if e + 1 < energies:
                         total = total + moved[e + 1]
-                    mixed[e, k, rows, columns] = total
+                    mixed[k, e, rows, columns] = total
             return carry
 
         lax.fori_loop(0, depth // 8, rows_of, 0, unroll=True)
@@ -440,11 +440,11 @@
     )
     group = energies * momenta
     depth = 2 * n // group
-    axes = ("energy", "momentum")
+    axes = ("momentum", "energy")
     spread = lax.all_to_all(
         greens.reshape(group, depth, n), axes, split_axis=0, concat_axis=0, tiled=True
     )
-    block = (energies, momenta, depth, n)
+    block = (momenta, energies, depth, n)
     mixed = pl.pallas_call(
         mix_kernel,
         out_shape=jax.ShapeDtypeStruct(block, F32),

time: 90.8 us -> 90.6 us (level)
  no operation moved by 1% of the time
where the time goes in v5:
time: 90.6 us; the launch traced here: 90.3 us
  blocking collectives  47 us (52%)
  Pallas kernels  30.1 us (33%)
  starting transfers between devices  10.3 us (11%)
  waiting for transfers between devices  1.74 us (2%)
  local copies, waits for them, and re-layouts  1.04 us (1%)
    pallas_call x8, Pallas kernels, call(): pl.pallas_call(kernel, out_shape=outs, in_specs=[spec(o) for o in operand...  29.2 us
    all_to_all x1, blocking collectives, body(): lax.all_to_all(greens.reshape(group, depth, n), axes, split_axis=0, conca...  25.8 us
    all_to_all x1, blocking collectives, body(): lax.all_to_all(mixed.reshape(group, depth, n), axes, split_axis=0, concat...  21.2 us
    ppermute x2, starting transfers between devices, ahead(): lax.ppermute(block, axis, [(i, i + 1) for i in range(first, lax.axis_size...  5.99 us
    ppermute x2, starting transfers between devices, swap(): return lax.ppermute(block, axis, route)  4.28 us
  transfers between devices with their start and end apart: 4, of which 1 were waited for; matrix products, arithmetic and copies ran while one was open for 0% of the time, Pallas kernels for 20%

profile of v5, /device:TPU:0, one launch (start us, length us, event | category | flops | bytes accessed | tf_op | source)
XLA Modules:
  0.0 90.3 jit_solution(7619291651967656892)
XLA Ops:
  0.0 7.8 %shard_map.65 = (bf16[768,768]{1,0:T(8,128)(2,1)S(1)}, bf16[768,768]{1,0:T(8,128)(2,1)S(1)}, bf16[768,768]{1,0:T(8,128)(2,1)S(1)}, bf16[768,768]{1,0:T(8,128)(2,...) custom-call(f32[1,2,1,2,384,384]{5,4,3,2,1,0:T(8,128)} %diag.1, ...), custom_call_target="tpu_custom_call" | custom-call | flops 30000001024 | bytes 1 | tf_op jit(solution)/shard_map/pallas_call | solution.py:371
  7.8 0.7 collective-permute-start
  8.5 3.7 %shard_map.66 = (bf16[384,768]{1,0:T(8,128)(2,1)S(1)}, bf16[384,768]{1,0:T(8,128)(2,1)S(1)}, f32[384,768]{1,0:T(8,128)S(1)}) custom-call(f32[2,384,384]{2,1,0:T(8,128)S(1)} %get-tuple-element.28.even, bf16[768,768]{1,0:T(8,128)(2,1)S(1)} %get-tuple-element.29.refs_0_, bf16[768,768]{1,0:T(8,128)(2,1)S(1)} %get-tuple-element.30.refs_1_, ...), custom_call_target="tpu_custom_call" | custom-call | flops 30000001024 | bytes 1 | tf_op jit(solution)/shard_map/pallas_call | solution.py:371
  12.2 3.5 %collective-permute-start.1 = (f32[384,768]{1,0:T(8,128)S(1)}, f32[384,768]{1,0:T(8,128)S(1)}, u32[]{:S(2)}, u32[]{:S(2)}) collective-permute-start(f32[384,768]{1,0:T(8,128)S(1)} %get-tuple-element.46.mine), channel_id=1, source_target_pairs={{0,16},{16,0},{32,48},{48,32},{64,80},{80,64},{96,112},{112,96},{1... | collective-permute-start | bytes 3538952 | tf_op jit(solution)/shard_map/ppermute | solution.py:387
  15.8 2.9 %shard_map.67 = (f32[384,768]{1,0:T(8,128)S(1)}, f32[384,768]{1,0:T(8,128)S(1)}) custom-call(bf16[384,768]{1,0:T(8,128)(2,1)S(1)} %get-tuple-element.38.refs_0_, bf16[384,768]{1,0:T(8,128)(2,1)S(1)} %get-tuple-element.39.refs_1_, bf16[768,768]{1,0:T(8,128)(2,1)S(1)} %get-tuple-element.40.refs_2_, bf16[768,768]{1,0:T(8,128)(2,1)S(1)} %get-tuple-element.41.refs_3_, ...), custom_call_target="tpu_custom_call" | custom-call | flops 30000001024 | bytes 1 | tf_op jit(solution)/shard_map/pallas_call | solution.py:371
  18.7 0.0 collective-permute-done.1.far
  18.7 5.3 %shard_map.68 = (f32[384,768]{1,0:T(8,128)S(1)}, f32[384,768]{1,0:T(8,128)S(1)}) custom-call(f32[384,768]{1,0:T(8,128)S(1)} %get-tuple-element.46.mine, f32[384,768]{1,0:T(8,128)S(1)} %collective-permute-done.1.far, f32[384,768]{1,0:T(8,128)S(1)} %get-tuple-element.44.one, f32[384,768]{1,0:T(8,128)S(1)} %get-tuple-element.45.two), custom_call_target="tpu_custom_call" | custom-call | flops 30000001024 | bytes 1 | tf_op jit(solution)/shard_map/pallas_call | solution.py:371
  24.0 0.7 collective-permute-start.2
  24.8 0.0 collective-permute-done.far
  24.8 0.0 copy-start
  24.8 0.0 copy-start.1
  24.8 0.0 copy-start.2
  24.8 0.0 copy-start.3
  24.8 5.3 %shard_map.69 = (f32[384,768]{1,0:T(8,128)S(1)}, f32[384,768]{1,0:T(8,128)S(1)}) custom-call(f32[384,768]{1,0:T(8,128)S(1)} %get-tuple-element.37.mine, f32[384,768]{1,0:T(8,128)S(1)} %collective-permute-done.far, f32[384,768]{1,0:T(8,128)S(1)} %get-tuple-element.44.one, f32[384,768]{1,0:T(8,128)S(1)} %get-tuple-element.45.two, ...), custom_call_target="tpu_custom_call" | custom-call | flops 30000001024 | bytes 1 | tf_op jit(solution)/shard_map/pallas_call | solution.py:371
  30.2 5.3 %collective-permute-start.3 = (f32[384,768]{1,0:T(8,128)S(1)}, f32[384,768]{1,0:T(8,128)S(1)}, u32[]{:S(2)}, u32[]{:S(2)}) collective-permute-start(f32[384,768]{1,0:T(8,128)S(1)} %get-tuple-element.50), channel_id=1, source_target_pairs={{0,16},{32,48},{64,80},{96,112},{1,17},{33,49},{65,81},{97,113},{2... | collective-permute-start | bytes 3538952 | tf_op jit(solution)/shard_map/ppermute | solution.py:391
  35.4 0.0 copy-done
  35.4 0.0 copy-done.1
  35.4 0.0 copy-done.2
  35.4 0.0 copy-done.3
  35.5 0.6 shard_map.64.weights
  36.1 1.7 %collective-permute-done.3.chip_term = f32[384,768]{1,0:T(8,128)S(1)} collective-permute-done((f32[384,768]{1,0:T(8,128)S(1)}, f32[384,768]{1,0:T(8,128)S(1)}, u32[]{:S(2)}, u32[]{:S(2)}) %collective-permute-start.3) | collective-permute-done | bytes 1179680 | tf_op jit(solution)/shard_map/ppermute | solution.py:391
  37.8 0.0 collective-permute-done.2.border_term
  37.8 3.6 %shard_map.71 = f32[2,384,384]{2,1,0:T(8,128)S(1)} custom-call(f32[384,768]{1,0:T(8,128)S(1)} %get-tuple-element.49.partial, f32[384,768]{1,0:T(8,128)S(1)} %collective-permute-done.2.border_term, f32[2,384,384]{2,1,0:T(8,128)S(1)} %shard_map.70.odd_greens), custom_call_target="tpu_custom_call", output_to_operand_aliasing={{}: (2, {})} | custom-call | flops 30000001024 | bytes 1 | tf_op jit(solution)/shard_map/pallas_call | solution.py:371
  41.4 25.8 %all_to_all.10 = f32[16,48,384]{2,1,0:T(8,128)S(1)} all-to-all(f32[16,48,384]{2,1,0:T(8,128)S(1)} %bitcast.6), channel_id=1, replica_groups=mesh['layer'=8,'energy'=4,'momentum'=4] {'momentum','energy'}, dimensions={0} | all-to-all | bytes 2359296 | tf_op jit(solution)/shard_map/all_to_all | solution.py:444
  67.2 0.9 shard_map.72
  68.0 21.2 %all_to_all.11 = f32[16,48,384]{2,1,0:T(8,128)S(1)} all-to-all(f32[16,48,384]{2,1,0:T(8,128)S(1)} %bitcast.5), channel_id=1, replica_groups=mesh['layer'=8,'energy'=4,'momentum'=4] {'momentum','energy'}, dimensions={0} | all-to-all | bytes 2359296 | tf_op jit(solution)/shard_map/all_to_all | solution.py:455
  89.3 1.0 %copy.10 = f32[1,1,1,2,384,384]{5,4,3,2,1,0:T(8,128)} copy(f32[1,1,1,2,384,384]{5,4,3,2,1,0:T(8,128)S(1)} %bitcast.7) | data formatting | bytes 2359296
  (1 shorter events, 0.0 us)
Async XLA Ops:
  7.8 17.0 %collective-permute-start = (f32[384,768]{1,0:T(8,128)S(1)}, f32[384,768]{1,0:T(8,128)S(1)}, u32[]{:S(2)}, u32[]{:S(2)}) collective-permute-start(f32[384,768]{1,0:T(8,128)S(1)} %get-tuple-element.37.mine), channel_id=1, source_target_pairs={{16,32},{32,16},{48,64},{64,48},{80,96},{96,80},{17,33},{33,17},{4... | collective-permute-start | bytes 3538952 | tf_op jit(solution)/shard_map/ppermute | solution.py:387
  12.2 6.5 %collective-permute-start.1 = (f32[384,768]{1,0:T(8,128)S(1)}, f32[384,768]{1,0:T(8,128)S(1)}, u32[]{:S(2)}, u32[]{:S(2)}) collective-permute-start(f32[384,768]{1,0:T(8,128)S(1)} %get-tuple-element.46.mine), channel_id=1, source_target_pairs={{0,16},{16,0},{32,48},{48,32},{64,80},{80,64},{96,112},{112,96},{1... | collective-permute-start | bytes 3538952 | tf_op jit(solution)/shard_map/ppermute | solution.py:387
  24.0 13.8 %collective-permute-start.2 = (f32[384,768]{1,0:T(8,128)S(1)}, f32[384,768]{1,0:T(8,128)S(1)}, u32[]{:S(2)}, u32[]{:S(2)}) collective-permute-start(f32[384,768]{1,0:T(8,128)S(1)} %get-tuple-element.48.chip_term), channel_id=1, source_target_pairs={{16,32},{48,64},{80,96},{17,33},{49,65},{81,97},{18,34},{50,66},{8... | collective-permute-start | bytes 3538952 | tf_op jit(solution)/shard_map/ppermute | solution.py:391
  24.8 10.6 %copy-start = (f32[4,4]{1,0:T(4,128)S(1)}, f32[4,4]{1,0:T(4,128)}, u32[]{:S(2)}) copy-start(f32[4,4]{1,0:T(4,128)} %phonon.1) | copy-start | bytes 196
  24.8 10.6 %copy-start.1 = (f32[3]{0:T(128)S(1)}, f32[3]{0:T(128)}, u32[]{:S(2)}) copy-start(f32[3]{0:T(128)} %strength.1) | copy-start | bytes 40
  24.8 10.6 %copy-start.2 = (s32[4]{0:T(128)S(1)}, s32[4]{0:T(128)}, u32[]{:S(2)}) copy-start(s32[4]{0:T(128)} %transfer.1) | copy-start | bytes 52
  24.8 10.6 %copy-start.3 = (s32[3]{0:T(128)S(1)}, s32[3]{0:T(128)}, u32[]{:S(2)}) copy-start(s32[3]{0:T(128)} %offset.1) | copy-start | bytes 40
  30.2 7.6 %collective-permute-start.3 = (f32[384,768]{1,0:T(8,128)S(1)}, f32[384,768]{1,0:T(8,128)S(1)}, u32[]{:S(2)}, u32[]{:S(2)}) collective-permute-start(f32[384,768]{1,0:T(8,128)S(1)} %get-tuple-element.50), channel_id=1, source_target_pairs={{0,16},{32,48},{64,80},{96,112},{1,17},{33,49},{65,81},{97,113},{2... | collective-permute-start | bytes 3538952 | tf_op jit(solution)/shard_map/ppermute | solution.py:391
